TPU v7x, 32 devices: a whole 2x2x4 slice. The times are simulated.
32 devices in a mesh: fibre: 4 (over z), cols: 8 (over y, x, core).
Axes of the slice: x: 2, y: 2, z: 4, core: 2. Of those that a mesh axis runs over, the one named last changes fastest.
Arguments:
- tensor: float32 [512, 8, 4, 2048], P('fibre', 'cols'), may hold values from -6 to 6
- initial: float32 [512, 64], replicated, may hold values from -6 to 6
Outputs:
- core_slab: float32 [64, 8, 4, 2048], P(None, 'cols', 'fibre')
- basis: float32 [512, 64], replicated
All inputs are finite; a program needn't handle non-finite values.
Results may differ from a plain program's by a relative error of at most 0.0002.
Values sent between devices are 32-bit elements; how exact they have to be, the bound alone decides.
No kernel may reach another device: no remote copies, remote signals or barrier semaphores. Data moves between devices by JAX's collectives and lax.ppermute only.
A program may use at most 64 MiB of HBM per device.

v0:
```python
import jax
import jax.numpy as jnp
from jax import lax
from jax.sharding import PartitionSpec as P

ITERS = 2


def orthonormal(product):
    squares = jnp.dot(product.T, product, precision=lax.Precision.HIGHEST)
    lower = jnp.linalg.cholesky(squares)
    return lax.linalg.triangular_solve(
        lower, product, left_side=False, lower=True, transpose_a=True
    )


def shards(tensor, initial):
    highest = lax.Precision.HIGHEST
    gathered = lax.all_to_all(tensor, "fibre", split_axis=2, concat_axis=0, tiled=True)
    modes = gathered.shape[0]
    width = gathered.shape[3]
    columns = gathered.reshape(modes, width)
    local_gram = jnp.dot(columns, columns.T, precision=highest)
    gram = lax.psum(local_gram, ("fibre", "cols"))
    basis = initial
    for step in range(ITERS):
        basis = orthonormal(jnp.dot(gram, basis, precision=highest))
    ranks = basis.shape[1]
    core_slab = jnp.dot(basis.T, columns, precision=highest).reshape(ranks, 1, 1, width)
    return (core_slab, basis)


def solution(mesh):
    placed = (P("fibre", "cols", None, None), P())
    return jax.shard_map(
        shards,
        mesh=mesh,
        in_specs=placed,
        out_specs=(P(None, "cols", "fibre", None), P()),
        check_vma=False,
    )
```

profile of v0, /device:TPU:0, one launch (start us, length us, event | category | flops | bytes accessed | tf_op | source)
XLA Modules:
  0.0 294.8 jit_solution(3393844328094002086)
XLA Ops:
  7.2 0.0 copy-start
  7.2 0.0 all-reduce.2.cloned.1.call-start
  7.2 4.6 %copy.11 = f32[128,1,4,2048]{3,0,1,2:T(8,128)S(1)} copy(f32[128,1,4,2048]{3,2,1,0:T(4,128)} %param.5) | data formatting | bytes 8388608 | tf_op args[0]
  11.9 99.3 %all_to_all.15 = f32[128,1,4,2048]{3,0,1,2:T(8,128)S(1)} all-to-all(f32[128,1,4,2048]{3,0,1,2:T(8,128)S(1)} %copy.11), channel_id=1, replica_groups=mesh['fibre'=4,'cols'=8] {'fibre'}, dimensions={2} | all-to-all | bytes 8388608 | tf_op jit(solution)/shard_map/all_to_all | solution.py:19
  111.2 0.0 copy-start.1
  111.2 1.9 copy-done.1
  113.1 7.9 %fusion.8 = f32[512,512]{1,0:T(8,128)} fusion(f32[512,2048]{1,0:T(8,128)S(1)} %bitcast.43), kind=kOutput, calls=%fused_computation.20 | convolution fusion | flops 6442450944 | bytes 5242880 | tf_op jit(solution)/shard_map/dot_general | solution.py:23
  121.0 0.0 all-reduce.2.cloned.1.call-update
  121.0 130.2 %all-reduce.2.cloned.1.call-done = f32[512,512]{1,0:T(8,128)} async-done(((f32[512,512]{1,0:T(8,128)}), f32[512,512]{1,0:T(8,128)}) %all-reduce.2.cloned.1.call-update) | async-done | bytes 1048592 | tf_op jit(solution)/shard_map/psum | solution.py:24
  251.3 0.0 copy-done
  251.3 2.4 fusion.9
  253.6 0.3 fusion.10
  253.9 0.1 copy.12
  254.0 5.8 %cholesky.44 = f32[64,64]{1,0:T(8,128)S(1)} custom-call(f32[64,64]{1,0:T(8,128)S(1)} %fusion.5), custom_call_target="Cholesky" | custom-call | tf_op jit(solution)/shard_map/jit(cholesky)/cholesky | solution.py:11
  259.9 0.6 compare_reduce_fusion.1
  260.5 0.7 fusion
  261.2 4.9 %custom-call.6 = f32[1,64,64]{1,2,0:T(8,128)S(1)} custom-call(f32[1,64,64]{2,1,0:T(8,128)S(1)} %fusion), custom_call_target="InvertDiagBlocksLowerTriangular" | custom-call | tf_op jit(solution)/shard_map/triangular_solve/custom-call.0 | solution.py:12
  266.1 0.3 convolution_bitcast_fusion.2
  266.4 2.4 fusion.11
  268.8 0.3 fusion.12
  269.0 0.1 copy.13
  269.1 6.0 %cholesky.55 = f32[64,64]{1,0:T(8,128)S(1)} custom-call(f32[64,64]{1,0:T(8,128)S(1)} %fusion.3), custom_call_target="Cholesky" | custom-call | tf_op jit(solution)/shard_map/jit(cholesky)/cholesky | solution.py:11
  275.2 0.6 compare_reduce_fusion
  275.8 0.7 fusion.1
  276.5 4.9 %custom-call.7 = f32[1,64,64]{1,2,0:T(8,128)S(1)} custom-call(f32[1,64,64]{2,1,0:T(8,128)S(1)} %fusion.1), custom_call_target="InvertDiagBlocksLowerTriangular" | custom-call | tf_op jit(solution)/shard_map/triangular_solve/custom-call.0 | solution.py:12
  281.4 0.3 convolution_bitcast_fusion.1
  281.7 0.0 copy-start.2
  281.8 4.9 %convolution_bitcast_fusion = f32[64,1,1,2048]{3,0,2,1:T(8,128)S(1)} fusion(f32[512,64]{0,1:T(8,128)S(1)} %convolution_bitcast_fusion.1, f32[512,2048]{1,0:T(8,128)} %bitcast.44), kind=kOutput, calls=%fused_computation | convolution fusion | flops 805306368 | bytes 4849664 | tf_op jit(solution)/shard_map/dot_general | solution.py:29
  286.6 1.3 copy.14
  288.0 0.0 copy-done.2
  (4 shorter events, 0.1 us)
Async XLA Ops:
  7.2 244.1 %copy-start = (f32[512,64]{0,1:T(8,128)S(1)}, f32[512,64]{0,1:T(8,128)}, u32[]{:S(2)}) copy-start(f32[512,64]{0,1:T(8,128)} %param.6) | copy-start | bytes 393220
  7.2 244.1 %all-reduce.2.cloned.1.call-start = ((), (), s32[]{:S(2)}) async-start(), calls=%async_computation.1 | async-start | bytes 2097152 | tf_op jit(solution)/shard_map/psum | solution.py:24
  111.2 1.9 copy-start.1
  281.7 6.2 %copy-start.2 = (f32[512,64]{0,1:T(8,128)}, f32[512,64]{0,1:T(8,128)S(1)}, u32[]{:S(2)}) copy-start(f32[512,64]{0,1:T(8,128)S(1)} %convolution_bitcast_fusion.1) | copy-start | bytes 393220
Sparse Core Ops, SparseCore 0:
  121.2 130.0 all-reduce.1
where the time goes:
time: 295 us
  waiting for transfers between devices  130 us (44%)
  blocking collectives  99.3 us (34%)
  other arithmetic  24.4 us (8%)
  matrix products  18.7 us (6%)
  between operations  14.1 us (5%)
  local copies, waits for them, and re-layouts  8.07 us (3%)
    psum x1, waiting for transfers between devices, shards(): gram = lax.psum(local_gram, ('fibre', 'cols'))  130 us
    all_to_all x1, blocking collectives, shards(): lax.all_to_all(tensor, 'fibre', split_axis=2, concat_axis=0, tiled=True)  99.3 us
    another operation x6, other arithmetic, orthonormal(): lower = jnp.linalg.cholesky(squares)  13.2 us
    another operation x4, other arithmetic, orthonormal(): lax.linalg.triangular_solve(lower, product, left_side=False, lower=True,...  11.1 us
    dot_general x1, matrix products, shards(): local_gram = jnp.dot(columns, columns.T, precision=highest)  7.93 us
    unnamed x8, local copies, waits for them, and re-layouts  7.92 us
  transfers between devices with their start and end apart: 1, of which 1 were waited for; matrix products, arithmetic and copies ran while one was open for 0% of the time, Pallas kernels for 0%

commit v1 on v0

v1 whole, which is shorter than its diff:
```python
import functools
import itertools

import jax
import jax.numpy as jnp
from jax import lax
from jax.experimental import pallas as pl
from jax.experimental.pallas import tpu as pltpu
from jax.sharding import PartitionSpec as P


HIGHEST = lax.Precision.HIGHEST
VMEM = pl.BlockSpec(memory_space=pltpu.VMEM)
ANY = pl.BlockSpec(memory_space=pl.ANY)
ELIMINATE = 8
PROJECT = 512


def params(mib):
    return pltpu.CompilerParams(vmem_limit_bytes=mib << 20)


def f32(*shape):
    return jax.ShapeDtypeStruct(shape, jnp.float32)


def bf16(*shape):
    return jax.ShapeDtypeStruct(shape, jnp.bfloat16)


def dot(a, b, contract, precision=None):
    return lax.dot_general(
        a, b, (contract, ((), ())), precision=precision, preferred_element_type=jnp.float32
    )


NN = ((1,), (0,))
NT = ((1,), (1,))


def halves(value):
    high = value.astype(jnp.bfloat16)
    return high, (value - high.astype(jnp.float32)).astype(jnp.bfloat16)


def dot3(a, b, contract):
    return dot(a[0], b[0], contract) + (dot(a[0], b[1], contract) + dot(a[1], b[0], contract))


def eye(n):
    return jnp.where(
        lax.broadcasted_iota(jnp.int32, (n, n), 0) == lax.broadcasted_iota(jnp.int32, (n, n), 1), 1.0, 0.0
    ).astype(jnp.float32)


def inverse_factor(squares):
    n = squares.shape[0]
    wide = 2 * n
    step = ELIMINATE
    start = jnp.concatenate([squares, eye(n)], axis=1)
    rows = [start[i : i + step] for i in range(0, n, step)]
    below = lax.broadcasted_iota(jnp.int32, (step, wide), 0)
    for t in range(n // step):
        columns = [
            {i: jnp.broadcast_to(rows[i][:, t * step + j : t * step + j + 1], (step, wide)) for i in range(t, n // step)}
            for j in range(step)
        ]
        pivots = [rows[t][j : j + 1, :] for j in range(step)]
        update = {}
        for j in range(step):
            inverse = 1.0 / columns[j][t][j : j + 1, :]
            scaled = {i: columns[j][i] * inverse for i in range(t, n // step)}
            scaled[t] = jnp.where(below > j, scaled[t], 0.0)
            for i in range(t, n // step):
                term = scaled[i] * pivots[j]
                update[i] = update[i] + term if i in update else term
            for m in range(j + 1, step):
                pivots[m] = pivots[m] - scaled[t][m : m + 1, :] * pivots[j]
                across = columns[m][t][j : j + 1, :]
                for i in range(t, n // step):
                    columns[m][i] = columns[m][i] - scaled[i] * across
        for i in range(t, n // step):
            rows[i] = rows[i] - update[i]
    done = jnp.concatenate(rows, axis=0)
    left, right = done[:, :n], done[:, n:]
    diagonal = jnp.sum(left * eye(n), axis=1, keepdims=True)
    return right * lax.rsqrt(diagonal)


def extract_kernel(shift, column, tensor_ref, out_ref, sem):
    width = out_ref.shape[1]
    which = lax.axis_index("fibre") ^ shift
    copy = pltpu.make_async_copy(tensor_ref.at[:, 0, which, pl.ds(column, width)], out_ref, sem)
    copy.start()
    copy.wait()


def extract(shift, tensor, column, width):
    rows = tensor.shape[0]
    return pl.pallas_call(
        functools.partial(extract_kernel, shift, column),
        out_shape=f32(rows, width),
        in_specs=[ANY],
        out_specs=VMEM,
        scratch_shapes=[pltpu.SemaphoreType.DMA(())],
        compiler_params=params(62),
        cost_estimate=pl.CostEstimate(flops=0, bytes_accessed=8 * rows * width, transcendentals=0),
        name="extract",
    )(tensor)


def cross(every, new):
    size, rows = every[0].shape[0], new[0].shape[0]
    full = dot(jnp.concatenate(every, axis=0), jnp.concatenate(new, axis=0), NT)
    return full[:size, :rows] + (full[:size, rows:] + full[size:, :rows] + full[size:, rows:])


def joined(refs, columns=slice(None)):
    return tuple(jnp.concatenate([refs[k + s][:, columns] for k in range(0, len(refs), 2)], axis=0) for s in range(2))


def in_turn(ref, shifts):
    me = lax.axis_index("fibre")
    return jnp.concatenate([ref[me ^ shift] for shift in shifts], axis=1)


def low_core():
    return lax.axis_index("cols") % 2 == 0


def put(value, shifts, mine_ref, other_ref):
    me = lax.axis_index("fibre")
    half, rows = mine_ref.shape[1:]
    low, high = value[:half], value[half:]
    mine, other = jnp.where(low_core(), low, high), jnp.where(low_core(), high, low)
    for p, shift in enumerate(shifts):
        mine_ref[me ^ shift] = mine[:, p * rows : (p + 1) * rows]
        other_ref[me ^ shift] = other[:, p * rows : (p + 1) * rows]


def merged(mine, other):
    return jnp.concatenate([jnp.where(low_core(), mine, other), jnp.where(low_core(), other, mine)], axis=0)


def by_fibre(ref):
    return jnp.concatenate([ref[f] for f in range(ref.shape[0])], axis=1)


def arrive_kernel(parts, shifts, *refs):
    before = len(shifts) - 1
    piece = jnp.concatenate([ref[...] for ref in refs[:parts]], axis=1)
    basis_ref = refs[parts]
    old = refs[parts + 1 : parts + 1 + 2 * before]
    high_ref, low_ref, gram_ref, image_ref = refs[-4:]
    rows = piece.shape[0]
    new = halves(piece)
    high_ref[...], low_ref[...] = new
    if not before:
        every = new
    else:
        every = tuple(jnp.concatenate(pair, axis=0) for pair in zip(joined(old), new))
    column = cross(every, new)
    split = halves(column)
    basis = halves(in_turn(basis_ref, shifts))
    own = dot3(basis, split, NN)
    if not before:
        gram_ref[...] = column
        image_ref[...] = own
        return
    gram, image = refs[parts + 1 + 2 * before :][:2]
    side = before * rows
    mine = tuple(b[:, side:] for b in basis)
    earlier = dot3(mine, tuple(s[:side] for s in split), NT)
    image_ref[...] = jnp.concatenate([image[...] + earlier, own], axis=1)
    gram_ref[...] = jnp.concatenate(
        [jnp.concatenate([gram[...], column[:side].T], axis=0), column], axis=1
    )


def arrive(parts, shifts, basis, old, state):
    rows, width = parts[0].shape[0], sum(part.shape[1] for part in parts)
    size = len(shifts) * rows
    return pl.pallas_call(
        functools.partial(arrive_kernel, len(parts), shifts),
        out_shape=(bf16(rows, width), bf16(rows, width), f32(size, size), f32(basis.shape[1], size)),
        in_specs=[VMEM] * (len(parts) + 1 + len(old) + len(state)),
        out_specs=(VMEM,) * 4,
        compiler_params=params(24),
        cost_estimate=pl.CostEstimate(
            flops=8 * rows * width * size, bytes_accessed=4 * width * size, transcendentals=0
        ),
        name="arrive",
    )(*parts, basis, *old, *state)


def partial_kernel(start, *refs):
    piece_ref, old, (high_ref, low_ref, out_ref) = refs[0], refs[1:-3], refs[-3:]
    new = halves(piece_ref[...])
    high_ref[...], low_ref[...] = new
    every = tuple(
        jnp.concatenate(pair, axis=0) for pair in zip(joined(old, slice(start, start + new[0].shape[1])), new)
    )
    out_ref[...] = cross(every, new)


def partial_column(part, start, old):
    rows, width = part.shape
    size = (len(old) // 2 + 1) * rows
    return pl.pallas_call(
        functools.partial(partial_kernel, start),
        out_shape=(bf16(rows, width), bf16(rows, width), f32(size, rows)),
        in_specs=[VMEM] * (1 + len(old)),
        out_specs=(VMEM,) * 3,
        compiler_params=params(24),
        cost_estimate=pl.CostEstimate(
            flops=8 * rows * width * size, bytes_accessed=4 * width * size, transcendentals=0
        ),
        name="partial",
    )(part, *old)


def finish_kernel(start, shifts, piece_ref, basis_ref, image_ref, sofar_ref, *refs):
    old, (high_ref, low_ref, column_ref, mine_ref, other_ref) = refs[:-5], refs[-5:]
    rows = piece_ref.shape[0]
    new = halves(piece_ref[...])
    high_ref[...], low_ref[...] = new
    every = tuple(
        jnp.concatenate(pair, axis=0) for pair in zip(joined(old, slice(start, start + new[0].shape[1])), new)
    )
    column = sofar_ref[...] + cross(every, new)
    column_ref[...] = column
    side = column.shape[0] - rows
    split = halves(column)
    basis = halves(in_turn(basis_ref, shifts))
    own = dot3(basis, split, NN)
    earlier = image_ref[...] + dot3(tuple(b[:, side:] for b in basis), tuple(s[:side] for s in split), NT)
    put(jnp.concatenate([earlier, own], axis=1), shifts, mine_ref, other_ref)


def finish(part, start, shifts, basis, image, sofar, old):
    rows, width = part.shape
    size = sofar.shape[0]
    share = f32(len(shifts), basis.shape[1] // 2, rows)
    return pl.pallas_call(
        functools.partial(finish_kernel, start, shifts),
        out_shape=(bf16(rows, width), bf16(rows, width), f32(size, rows), share, share),
        in_specs=[VMEM] * (4 + len(old)),
        out_specs=(VMEM,) * 5,
        compiler_params=params(24),
        cost_estimate=pl.CostEstimate(
            flops=8 * rows * width * size, bytes_accessed=4 * width * size, transcendentals=0
        ),
        name="finish",
    )(part, basis, image, sofar, *old)


def second_kernel(shifts, mine_ref, other_ref, gram_ref, column_ref, to_mine_ref, to_other_ref):
    side = gram_ref.shape[0]
    image = halves(merged(in_turn(mine_ref, shifts), in_turn(other_ref, shifts)))
    gram = halves(gram_ref[...])
    column = halves(column_ref[...])
    late = dot3(image, column, NN)
    early = dot3(tuple(v[:, :side] for v in image), gram, NN)
    early = early + dot3(tuple(v[:, side:] for v in image), tuple(v[:side] for v in column), NT)
    put(jnp.concatenate([early, late], axis=1), shifts, to_mine_ref, to_other_ref)


def second(shifts, mine, other, gram, column):
    return pl.pallas_call(
        functools.partial(second_kernel, shifts),
        out_shape=(f32(*mine.shape), f32(*mine.shape)),
        in_specs=[VMEM] * 4,
        out_specs=(VMEM,) * 2,
        compiler_params=params(16),
        name="second",
    )(mine, other, gram, column)


def factor_kernel(mine_ref, other_ref, out_ref):
    image = merged(by_fibre(mine_ref), by_fibre(other_ref))
    out_ref[...] = inverse_factor(dot(image, image, NT, HIGHEST))


def factor(mine, other):
    ranks = 2 * mine.shape[1]
    return pl.pallas_call(
        factor_kernel,
        out_shape=f32(ranks, ranks),
        in_specs=[VMEM] * 2,
        out_specs=VMEM,
        compiler_params=params(8),
        cost_estimate=pl.CostEstimate(flops=40 * ranks**3, bytes_accessed=8 * mine.size, transcendentals=0),
        name="factor",
    )(mine, other)


def close_kernel(places, shifts, mine_ref, other_ref, inverse_ref, *refs):
    pieces, (core_ref, basis_ref, slab, sems) = refs[: 2 * len(places)], refs[2 * len(places) :]
    first = inverse_ref[...]
    image = dot(first, merged(by_fibre(mine_ref), by_fibre(other_ref)), NN, HIGHEST)
    turned = dot(first, merged(in_turn(mine_ref, shifts), in_turn(other_ref, shifts)), NN, HIGHEST)
    parts = halves(turned)
    inverse = inverse_factor(dot(image, image, NT, HIGHEST))
    width = core_ref.shape[3]
    chunk = min(PROJECT, width)
    raw = []
    for c in range(0, width, chunk):
        cut = [
            i for p in range(len(shifts)) for i, (q, at) in enumerate(places)
            if q == p and at <= c < at + pieces[2 * i].shape[1]
        ]
        columns = tuple(
            jnp.concatenate([pieces[2 * i + s][:, c - places[i][1] : c - places[i][1] + chunk] for i in cut], axis=0)
            for s in range(2)
        )
        raw.append(dot3(parts, columns, NN))
    basis_ref[...] = dot(inverse, image, NN, HIGHEST)
    split = halves(inverse)
    stores = []
    for n, c in enumerate(range(0, width, chunk)):
        slab[:, c : c + chunk] = dot3(split, halves(raw[n]), NN)
        stores.append(
            pltpu.make_async_copy(slab.at[:, pl.ds(c, chunk)], core_ref.at[:, 0, 0, pl.ds(c, chunk)], sems.at[n])
        )
        stores[-1].start()
    for store in stores:
        store.wait()


def close(shifts, mine, other, inverse, pieces, places, width):
    fibres, half, rows = mine.shape
    return pl.pallas_call(
        functools.partial(close_kernel, places, shifts),
        out_shape=(f32(2 * half, 1, 1, width), f32(2 * half, fibres * rows)),
        in_specs=[VMEM] * (3 + len(pieces)),
        out_specs=(ANY, VMEM),
        scratch_shapes=[
            pltpu.VMEM((2 * half, width), jnp.float32),
            pltpu.SemaphoreType.DMA((width // min(PROJECT, width),)),
        ],
        compiler_params=params(24),
        name="close",
    )(mine, other, inverse, *pieces)


def swap(value, axis, size, bit):
    return lax.ppermute(value, axis, [(i, i ^ bit) for i in range(size)])


def bits(size):
    return [1 << b for b in range(size.bit_length() - 1)]


def chips(n_fibre, n_cols):
    moves = [(0, bit) for bit in bits(n_cols)[1:]], [(bit, 0) for bit in bits(n_fibre)]
    return [axis[i : i + 2] for axis in moves for i in range(0, len(axis), 2)]


def across(value, n_fibre, n_cols, flip):
    perm = [
        (f * n_cols + c, (f ^ flip[0]) * n_cols + (c ^ flip[1])) for f in range(n_fibre) for c in range(n_cols)
    ]
    return lax.ppermute(value, ("fibre", "cols"), perm)


def total(mine, other, n_fibre, n_cols):
    mine = mine + swap(other, "cols", n_cols, 1)
    for flips in chips(n_fibre, n_cols):
        if len(flips) == 1:
            mine = mine + across(mine, n_fibre, n_cols, flips[0])
            continue
        both = (flips[0][0] ^ flips[1][0], flips[0][1] ^ flips[1][1])
        one, two, three = (across(mine, n_fibre, n_cols, flip) for flip in (*flips, both))
        mine = (mine + one) + (two + three)
    return mine, swap(mine, "cols", n_cols, 1)


def turns(n_fibre):
    images = [n_fibre - 1] + bits(n_fibre)[:-1]
    out = []
    for p in range(n_fibre):
        shift = 0
        for b, image in enumerate(images):
            shift ^= image if p >> b & 1 else 0
        out.append(shift)
    return out


def shards(n_fibre, n_cols, tensor, initial):
    rows, width = tensor.shape[0], tensor.shape[3]
    shifts = turns(n_fibre)
    start = initial.reshape(n_fibre, rows, initial.shape[1]).transpose(0, 2, 1)

    tail = width - width // 4
    last = n_fibre - 1
    cuts = {1: (0, width // 2, width), last: (0, tail, width)}
    parts, sends = {}, 0
    for p in [*range(1, last), 0, last]:
        parts[p] = []
        for c, end in itertools.pairwise(cuts.get(p, (0, width))):
            part = extract(shifts[p], tensor, c, end - c)
            if p:
                part = swap(part, "fibre", n_fibre, shifts[p])
                sends += 1
            parts[p].append(part)

    old, state, places = (), (), []
    for p in range(last):
        high, low, gram, image = arrive(parts[p], shifts[: p + 1], start, old, state)
        old += (high, low)
        state = (gram, image)
        places.append((p, 0))
    high, low, column = partial_column(parts[last][0], 0, old)
    *ends, column, mine, other = finish(parts[last][1], tail, shifts, start, image, column, old)
    pieces = (*old, high, low, *ends)
    places += [(last, 0), (last, tail)]

    mine, other = total(mine, other, n_fibre, n_cols)
    inverse = factor(mine, other)
    mine, other = total(*second(shifts, mine, other, gram, column), n_fibre, n_cols)
    core_slab, basis_t = close(shifts, mine, other, inverse, pieces, places, width)
    return (core_slab, basis_t.T)


def solution(mesh):
    n_fibre, n_cols = mesh.shape["fibre"], mesh.shape["cols"]
    placed = (P("fibre", "cols", None, None), P())

    def body(tensor, initial):
        return shards(n_fibre, n_cols, tensor, initial)

    return jax.shard_map(
        body,
        mesh=mesh,
        in_specs=placed,
        out_specs=(P(None, "cols", "fibre", None), P()),
        check_vma=False,
    )
```

time: 295 us -> 148 us (0.50)
  blocking collectives: 99.3 us -> 0 us
  waiting for transfers between devices: 130 us -> 91.3 us
  Pallas kernels: 0 us -> 27.6 us
  starting transfers between devices: 0.04 us -> 26.3 us
  other arithmetic: 24.4 us -> 0.1 us
  matrix products: 18.7 us -> 0 us
  between operations: 14.1 us -> 0.83 us
  local copies, waits for them, and re-layouts: 8.07 us -> 1.24 us
    psum x1 -> x0, waiting for transfers between devices: 130 us -> none  [shards(): gram = lax.psum(local_gram, ('fibre', 'cols'))]
    all_to_all x1 -> x0, blocking collectives: 99.3 us -> none  [shards(): lax.all_to_all(tensor, 'fibre', split_axis=2, concat_axis=0, tiled=True)]
    ppermute x0 -> x21, waiting for transfers between devices: none -> 91.3 us  [the longest x9 74.8 us: swap(): return lax.ppermute(value, axis, [(i, i ^ bit) for i in range(size)])]
    pallas_call x0 -> x14, Pallas kernels: none -> 27.6 us  [the longest x6 12 us: extract(): pl.pallas_call(functools.partial(extract_kernel, shift, column), out_shap...]
    ppermute x0 -> x21, starting transfers between devices: none -> 26.3 us  [the longest x12 16.1 us: across(): return lax.ppermute(value, ('fibre', 'cols'), perm)]
    another operation x10 -> x0, other arithmetic: 24.3 us -> none  [the longest x6 13.2 us: orthonormal(): lower = jnp.linalg.cholesky(squares)]
    dot_general x6 -> x0, matrix products: 18 us -> none  [the longest x1 7.93 us: shards(): local_gram = jnp.dot(columns, columns.T, precision=highest)]
    unnamed x8 -> x4, local copies, waits for them, and re-layouts: 7.92 us -> 1.23 us
  transfers between devices with their start and end apart: 1 -> 21, of which waited for: 1 -> 17; matrix products, arithmetic and copies ran while one was open for 0% -> 0% of each run, Pallas kernels for 0% -> 12%
where the time goes in v1:
time: 148 us; the launch traced here: 147 us
  waiting for transfers between devices  91.3 us (62%)
  Pallas kernels  27.6 us (19%)
  starting transfers between devices  26.3 us (18%)
    ppermute x9, waiting for transfers between devices, swap(): return lax.ppermute(value, axis, [(i, i ^ bit) for i in range(size)])  74.8 us
    ppermute x12, waiting for transfers between devices, across(): return lax.ppermute(value, ('fibre', 'cols'), perm)  16.4 us
    ppermute x12, starting transfers between devices, across(): return lax.ppermute(value, ('fibre', 'cols'), perm)  16.1 us
    pallas_call x6, Pallas kernels, extract(): pl.pallas_call(functools.partial(extract_kernel, shift, column), out_shap...  12 us
    ppermute x9, starting transfers between devices, swap(): return lax.ppermute(value, axis, [(i, i ^ bit) for i in range(size)])  10.2 us
    pallas_call x1, Pallas kernels, close(): pl.pallas_call(functools.partial(close_kernel, places, shifts), out_shape...  4.57 us
    pallas_call x3, Pallas kernels, arrive(): pl.pallas_call(functools.partial(arrive_kernel, len(parts), shifts), out_...  4.26 us
  transfers between devices with their start and end apart: 21, of which 17 were waited for; matrix products, arithmetic and copies ran while one was open for 0% of the time, Pallas kernels for 12%

profile of v1, /device:TPU:0, one launch (start us, length us, event | category | flops | bytes accessed | tf_op | source)
XLA Modules:
  0.0 147.3 jit_solution(751657697782904940)
XLA Ops:
  0.6 0.0 copy-start
  0.6 2.3 %extract.7 = f32[128,2048]{1,0:T(8,128)} custom-call(f32[128,1,4,2048]{3,2,1,0:T(4,128)} %tensor_ref.11), custom_call_target="tpu_custom_call" | custom-call | bytes 2097152 | tf_op jit(solution)/shard_map/extract/pallas_call | solution.py:100
  3.0 3.1 %collective-permute-start.1 = (f32[128,2048]{1,0:T(8,128)}, f32[128,2048]{1,0:T(8,128)S(1)}, u32[]{:S(2)}, u32[]{:S(2)}) collective-permute-start(f32[128,2048]{1,0:T(8,128)} %extract.7), channel_id=1, source_target_pairs={{0,8},{8,0},{16,24},{24,16},{1,9},{9,1},{17,25},{25,17},{2,10},{10... | collective-permute-start | bytes 3145736 | tf_op jit(solution)/shard_map/ppermute | solution.py:347
  6.1 2.1 %extract.11 = f32[128,1536]{1,0:T(8,128)} custom-call(f32[128,1,4,2048]{3,2,1,0:T(4,128)} %tensor_ref.11), custom_call_target="tpu_custom_call" | custom-call | bytes 1572864 | tf_op jit(solution)/shard_map/extract/pallas_call | solution.py:100
  8.1 2.7 %collective-permute-start.4 = (f32[128,1536]{1,0:T(8,128)}, f32[128,1536]{1,0:T(8,128)}, u32[]{:S(2)}, u32[]{:S(2)}) collective-permute-start(f32[128,1536]{1,0:T(8,128)} %extract.11), channel_id=1, source_target_pairs={{0,16},{8,24},{16,0},{24,8},{1,17},{9,25},{17,1},{25,9},{2,18},{10... | collective-permute-start | bytes 2359304 | tf_op jit(solution)/shard_map/ppermute | solution.py:347
  10.8 1.9 %extract.9 = f32[128,1024]{1,0:T(8,128)} custom-call(f32[128,1,4,2048]{3,2,1,0:T(4,128)} %tensor_ref.11), custom_call_target="tpu_custom_call" | custom-call | bytes 1048576 | tf_op jit(solution)/shard_map/extract/pallas_call | solution.py:100
  12.7 0.1 collective-permute-start.2
  12.8 1.9 %extract.10 = f32[128,1024]{1,0:T(8,128)} custom-call(f32[128,1,4,2048]{3,2,1,0:T(4,128)} %tensor_ref.11), custom_call_target="tpu_custom_call" | custom-call | bytes 1048576 | tf_op jit(solution)/shard_map/extract/pallas_call | solution.py:100
  14.6 3.9 %collective-permute-start.3 = (f32[128,1024]{1,0:T(8,128)}, f32[128,1024]{1,0:T(8,128)}, u32[]{:S(2)}, u32[]{:S(2)}) collective-permute-start(f32[128,1024]{1,0:T(8,128)} %extract.10), channel_id=1, source_target_pairs={{0,24},{8,16},{16,8},{24,0},{1,25},{9,17},{17,9},{25,1},{2,26},{10... | collective-permute-start | bytes 1572872 | tf_op jit(solution)/shard_map/ppermute | solution.py:347
  18.5 1.7 %extract.6 = f32[128,512]{1,0:T(8,128)} custom-call(f32[128,1,4,2048]{3,2,1,0:T(4,128)} %tensor_ref.11), custom_call_target="tpu_custom_call" | custom-call | bytes 524288 | tf_op jit(solution)/shard_map/extract/pallas_call | solution.py:100
  20.2 0.1 collective-permute-start
  20.3 0.0 copy-done
  20.3 2.2 %extract.8.refs_0_ = f32[128,2048]{1,0:T(8,128)} custom-call(f32[128,1,4,2048]{3,2,1,0:T(4,128)} %tensor_ref.11), custom_call_target="tpu_custom_call" | custom-call | bytes 2097152 | tf_op jit(solution)/shard_map/extract/pallas_call | solution.py:100
  22.6 0.0 copy-start.1
  22.6 1.2 copy-done.1
  23.8 0.7 arrive.3
  24.5 36.5 %collective-permute-done.2.refs_0_ = f32[128,1024]{1,0:T(8,128)S(1)} collective-permute-done((f32[128,1024]{1,0:T(8,128)}, f32[128,1024]{1,0:T(8,128)S(1)}, u32[]{:S(2)}, u32[]{:S(2)}) %collective-permute-start.2) | collective-permute-done | bytes 524320 | tf_op jit(solution)/shard_map/ppermute | solution.py:347
  61.0 11.3 %collective-permute-done.3.refs_1_ = f32[128,1024]{1,0:T(8,128)} collective-permute-done((f32[128,1024]{1,0:T(8,128)}, f32[128,1024]{1,0:T(8,128)}, u32[]{:S(2)}, u32[]{:S(2)}) %collective-permute-start.3) | collective-permute-done | bytes 524320 | tf_op jit(solution)/shard_map/ppermute | solution.py:347
  72.3 2.1 %arrive.4 = (bf16[128,2048]{1,0:T(8,128)(2,1)S(1)}, bf16[128,2048]{1,0:T(8,128)(2,1)S(1)}, f32[256,256]{1,0:T(8,128)S(1)}, f32[64,256]{1,0:T(8,128)S(1)}) custom-call(f32[128,1024]{1,0:T(8,128)S(1)} %collective-permute-done.2.refs_0_, f32[128,1024]{1,0:T(8,128)} %collective-permute-done.3.refs_1_, ...), custom_call_target="tpu_custom_call" | custom-call | flops 536870912 | bytes 2097152 | tf_op jit(solution)/shard_map/arrive/pallas_call | solution.py:183
  74.4 0.0 collective-permute-done.1.refs_0_
  74.5 1.4 arrive.5
  75.9 0.0 collective-permute-done.4.refs_0_
  75.9 2.2 %partial.1 = (bf16[128,1536]{1,0:T(8,128)(2,1)S(1)}, bf16[128,1536]{1,0:T(8,128)(2,1)S(1)}, f32[512,128]{1,0:T(8,128)S(1)}) custom-call(f32[128,1536]{1,0:T(8,128)} %collective-permute-done.4.refs_0_, bf16[128,2048]{1,0:T(8,128)(2,1)S(1)} %get-tuple-element.26.refs_3_.refs_2_.refs_1_.refs_0_, ...), custom_call_target="tpu_custom_call" | custom-call | flops 805306368 | bytes 3145728 | tf_op jit(solution)/shard_map/partial/pallas_call | solution.py:209
  78.1 23.4 %collective-permute-done.piece_ref = f32[128,512]{1,0:T(8,128)} collective-permute-done((f32[128,512]{1,0:T(8,128)}, f32[128,512]{1,0:T(8,128)}, u32[]{:S(2)}, u32[]{:S(2)}) %collective-permute-start) | collective-permute-done | bytes 262176 | tf_op jit(solution)/shard_map/ppermute | solution.py:347
  101.5 2.0 %finish.1 = (bf16[128,512]{1,0:T(8,128)(2,1)S(1)}, bf16[128,512]{1,0:T(8,128)(2,1)S(1)}, f32[512,128]{1,0:T(8,128)S(1)}, f32[4,32,128]{2,1,0:T(8,128)S(1)}, f32[4,32,128]{2,1,0:T(8,128)S(1)}) custom-call(f32[128,512]{1,0:T(8,128)} %collective-permute-done.piece_ref, f32[4,64,128]{2,1,0:T(8,128)S(1)} %bitcast_bitcast_fusion.refs_1_.refs_2_.basis_ref, ...), custom_call_target="tpu_custom_call" | custom-call | flops 268435456 | bytes 1048576 | tf_op jit(solution)/shard_map/finish/pallas_call | solution.py:244
  103.5 0.1 collective-permute-start.5
  103.5 1.2 collective-permute-done.5
  104.8 1.6 %collective-permute-start.6 = (f32[4,32,128]{2,1,0:T(8,128)S(1)}, f32[4,32,128]{2,1,0:T(8,128)S(1)}, u32[]{:S(2)}, u32[]{:S(2)}) collective-permute-start(f32[4,32,128]{2,1,0:T(8,128)S(1)} %add.42), channel_id=1, source_target_pairs={{0,2},{1,3},{2,0},{3,1},{4,6},{5,7},{6,4},{7,5},{8,10},{9,11},{10,... | collective-permute-start | bytes 196616 | tf_op jit(solution)/shard_map/ppermute | solution.py:363
  106.3 1.5 %collective-permute-start.7 = (f32[4,32,128]{2,1,0:T(8,128)S(1)}, f32[4,32,128]{2,1,0:T(8,128)S(1)}, u32[]{:S(2)}, u32[]{:S(2)}) collective-permute-start(f32[4,32,128]{2,1,0:T(8,128)S(1)} %add.42), channel_id=1, source_target_pairs={{0,4},{1,5},{2,6},{3,7},{4,0},{5,1},{6,2},{7,3},{8,12},{9,13},{10,... | collective-permute-start | bytes 196616 | tf_op jit(solution)/shard_map/ppermute | solution.py:363
  107.9 0.5 collective-permute-start.8
  108.3 0.8 collective-permute-done.6
  109.1 1.5 %collective-permute-done.7 = f32[4,32,128]{2,1,0:T(8,128)S(1)} collective-permute-done((f32[4,32,128]{2,1,0:T(8,128)S(1)}, f32[4,32,128]{2,1,0:T(8,128)S(1)}, u32[]{:S(2)}, u32[]{:S(2)}) %collective-permute-start.7) | collective-permute-done | bytes 65568 | tf_op jit(solution)/shard_map/ppermute | solution.py:363
  110.6 2.4 %collective-permute-done.8 = f32[4,32,128]{2,1,0:T(8,128)S(1)} collective-permute-done((f32[4,32,128]{2,1,0:T(8,128)S(1)}, f32[4,32,128]{2,1,0:T(8,128)S(1)}, u32[]{:S(2)}, u32[]{:S(2)}) %collective-permute-start.8) | collective-permute-done | bytes 65568 | tf_op jit(solution)/shard_map/ppermute | solution.py:363
  113.1 3.2 %collective-permute-start.10 = (f32[4,32,128]{2,1,0:T(8,128)S(1)}, f32[4,32,128]{2,1,0:T(8,128)S(1)}, u32[]{:S(2)}, u32[]{:S(2)}) collective-permute-start(f32[4,32,128]{2,1,0:T(8,128)S(1)} %add_add_fusion.3), channel_id=1, source_target_pairs={{0,16},{1,17},{2,18},{3,19},{4,20},{5,21},{6,22},{7,23},{8,24},{9,... | collective-permute-start | bytes 196616 | tf_op jit(solution)/shard_map/ppermute | solution.py:363
  116.2 1.3 collective-permute-start.11
  117.6 0.0 collective-permute-start.9
  117.6 0.9 collective-permute-done.10
  118.5 3.9 %collective-permute-done.11 = f32[4,32,128]{2,1,0:T(8,128)S(1)} collective-permute-done((f32[4,32,128]{2,1,0:T(8,128)S(1)}, f32[4,32,128]{2,1,0:T(8,128)S(1)}, u32[]{:S(2)}, u32[]{:S(2)}) %collective-permute-start.11) | collective-permute-done | bytes 65568 | tf_op jit(solution)/shard_map/ppermute | solution.py:363
  122.4 0.1 collective-permute-done.9
  122.6 0.1 collective-permute-start.12
  122.6 1.2 collective-permute-done.12.other_ref
  123.9 0.5 second.1
  124.4 0.2 collective-permute-start.13
  124.6 1.1 collective-permute-done.13
  125.7 0.6 collective-permute-start.14
  126.3 0.5 collective-permute-start.15
  126.8 2.4 %collective-permute-start.16 = (f32[4,32,128]{2,1,0:T(8,128)S(1)}, f32[4,32,128]{2,1,0:T(8,128)S(1)}, u32[]{:S(2)}, u32[]{:S(2)}) collective-permute-start(f32[4,32,128]{2,1,0:T(8,128)S(1)} %add.49), channel_id=1, source_target_pairs={{0,6},{1,7},{2,4},{3,5},{4,2},{5,3},{6,0},{7,1},{8,14},{9,15},{10,... | collective-permute-start | bytes 196616 | tf_op jit(solution)/shard_map/ppermute | solution.py:363
  129.2 0.8 collective-permute-done.14
  130.1 1.2 collective-permute-done.15
  131.3 0.7 collective-permute-done.16
  132.0 0.1 collective-permute-start.17
  132.1 2.3 %collective-permute-start.18 = (f32[4,32,128]{2,1,0:T(8,128)S(1)}, f32[4,32,128]{2,1,0:T(8,128)S(1)}, u32[]{:S(2)}, u32[]{:S(2)}) collective-permute-start(f32[4,32,128]{2,1,0:T(8,128)S(1)} %add_add_fusion.1), channel_id=1, source_target_pairs={{0,16},{1,17},{2,18},{3,19},{4,20},{5,21},{6,22},{7,23},{8,24},{9,... | collective-permute-start | bytes 196616 | tf_op jit(solution)/shard_map/ppermute | solution.py:363
  134.4 2.0 %collective-permute-start.19 = (f32[4,32,128]{2,1,0:T(8,128)S(1)}, f32[4,32,128]{2,1,0:T(8,128)S(1)}, u32[]{:S(2)}, u32[]{:S(2)}) collective-permute-start(f32[4,32,128]{2,1,0:T(8,128)S(1)} %add_add_fusion.1), channel_id=1, source_target_pairs={{0,24},{1,25},{2,26},{3,27},{4,28},{5,29},{6,30},{7,31},{8,16},{9,... | collective-permute-start | bytes 196616 | tf_op jit(solution)/shard_map/ppermute | solution.py:363
  136.4 0.0 collective-permute-done.17
  136.4 2.3 %collective-permute-done.18 = f32[4,32,128]{2,1,0:T(8,128)S(1)} collective-permute-done((f32[4,32,128]{2,1,0:T(8,128)S(1)}, f32[4,32,128]{2,1,0:T(8,128)S(1)}, u32[]{:S(2)}, u32[]{:S(2)}) %collective-permute-start.18) | collective-permute-done | bytes 65568 | tf_op jit(solution)/shard_map/ppermute | solution.py:363
  138.7 1.8 %collective-permute-done.19 = f32[4,32,128]{2,1,0:T(8,128)S(1)} collective-permute-done((f32[4,32,128]{2,1,0:T(8,128)S(1)}, f32[4,32,128]{2,1,0:T(8,128)S(1)}, u32[]{:S(2)}, u32[]{:S(2)}) %collective-permute-start.19) | collective-permute-done | bytes 65568 | tf_op jit(solution)/shard_map/ppermute | solution.py:363
  140.5 0.1 collective-permute-start.20
  140.6 2.1 %factor.1.inverse_ref = f32[64,64]{1,0:T(8,128)S(1)} custom-call(f32[4,32,128]{2,1,0:T(8,128)S(1)} %add_add_fusion.2.mine_ref, f32[4,32,128]{2,1,0:T(8,128)S(1)} %collective-permute-done.12.other_ref), custom_call_target="tpu_custom_call" | custom-call | flops 10485760 | bytes 131072 | tf_op jit(solution)/shard_map/factor/pallas_call | solution.py:286
  142.7 0.0 collective-permute-done.20.other_ref
  142.7 4.6 %close.1 = (f32[64,1,1,2048]{3,2,1,0:T(1,128)}, f32[64,512]{1,0:T(8,128)}) custom-call(f32[4,32,128]{2,1,0:T(8,128)S(1)} %add_add_fusion.mine_ref, f32[4,32,128]{2,1,0:T(8,128)S(1)} %collective-permute-done.20.other_ref, f32[64,64]{1,0:T(8,128)S(1)} %factor.1.inverse_ref, bf16[128,2048]{1,0:T(8,128)(2,1)S(1)} %get-tuple-element.26.refs_3_.refs_2_.refs_1_.refs_0_, ...), custom_call_target="tpu_custom_call" | custom-call | tf_op jit(solution)/shard_map/close/pallas_call | solution.py:332
  (7 shorter events, 0.1 us)
Async XLA Ops:
  0.6 19.7 %copy-start = (f32[512,64]{0,1:T(8,128)S(1)}, f32[512,64]{0,1:T(8,128)}, u32[]{:S(2)}) copy-start(f32[512,64]{0,1:T(8,128)} %param.3) | copy-start | bytes 393220
  3.0 71.5 %collective-permute-start.1 = (f32[128,2048]{1,0:T(8,128)}, f32[128,2048]{1,0:T(8,128)S(1)}, u32[]{:S(2)}, u32[]{:S(2)}) collective-permute-start(f32[128,2048]{1,0:T(8,128)} %extract.7), channel_id=1, source_target_pairs={{0,8},{8,0},{16,24},{24,16},{1,9},{9,1},{17,25},{25,17},{2,10},{10... | collective-permute-start | bytes 3145736 | tf_op jit(solution)/shard_map/ppermute | solution.py:347
  8.1 67.8 %collective-permute-start.4 = (f32[128,1536]{1,0:T(8,128)}, f32[128,1536]{1,0:T(8,128)}, u32[]{:S(2)}, u32[]{:S(2)}) collective-permute-start(f32[128,1536]{1,0:T(8,128)} %extract.11), channel_id=1, source_target_pairs={{0,16},{8,24},{16,0},{24,8},{1,17},{9,25},{17,1},{25,9},{2,18},{10... | collective-permute-start | bytes 2359304 | tf_op jit(solution)/shard_map/ppermute | solution.py:347
  12.7 48.3 %collective-permute-start.2 = (f32[128,1024]{1,0:T(8,128)}, f32[128,1024]{1,0:T(8,128)S(1)}, u32[]{:S(2)}, u32[]{:S(2)}) collective-permute-start(f32[128,1024]{1,0:T(8,128)} %extract.9), channel_id=1, source_target_pairs={{0,24},{8,16},{16,8},{24,0},{1,25},{9,17},{17,9},{25,1},{2,26},{10... | collective-permute-start | bytes 1572872 | tf_op jit(solution)/shard_map/ppermute | solution.py:347
  14.6 57.7 %collective-permute-start.3 = (f32[128,1024]{1,0:T(8,128)}, f32[128,1024]{1,0:T(8,128)}, u32[]{:S(2)}, u32[]{:S(2)}) collective-permute-start(f32[128,1024]{1,0:T(8,128)} %extract.10), channel_id=1, source_target_pairs={{0,24},{8,16},{16,8},{24,0},{1,25},{9,17},{17,9},{25,1},{2,26},{10... | collective-permute-start | bytes 1572872 | tf_op jit(solution)/shard_map/ppermute | solution.py:347
  20.2 81.3 %collective-permute-start = (f32[128,512]{1,0:T(8,128)}, f32[128,512]{1,0:T(8,128)}, u32[]{:S(2)}, u32[]{:S(2)}) collective-permute-start(f32[128,512]{1,0:T(8,128)} %extract.6), channel_id=1, source_target_pairs={{0,16},{8,24},{16,0},{24,8},{1,17},{9,25},{17,1},{25,9},{2,18},{10... | collective-permute-start | bytes 786440 | tf_op jit(solution)/shard_map/ppermute | solution.py:347
  22.6 1.2 copy-start.1
  103.5 1.3 collective-permute-start.5
  104.8 4.3 %collective-permute-start.6 = (f32[4,32,128]{2,1,0:T(8,128)S(1)}, f32[4,32,128]{2,1,0:T(8,128)S(1)}, u32[]{:S(2)}, u32[]{:S(2)}) collective-permute-start(f32[4,32,128]{2,1,0:T(8,128)S(1)} %add.42), channel_id=1, source_target_pairs={{0,2},{1,3},{2,0},{3,1},{4,6},{5,7},{6,4},{7,5},{8,10},{9,11},{10,... | collective-permute-start | bytes 196616 | tf_op jit(solution)/shard_map/ppermute | solution.py:363
  106.3 4.3 %collective-permute-start.7 = (f32[4,32,128]{2,1,0:T(8,128)S(1)}, f32[4,32,128]{2,1,0:T(8,128)S(1)}, u32[]{:S(2)}, u32[]{:S(2)}) collective-permute-start(f32[4,32,128]{2,1,0:T(8,128)S(1)} %add.42), channel_id=1, source_target_pairs={{0,4},{1,5},{2,6},{3,7},{4,0},{5,1},{6,2},{7,3},{8,12},{9,13},{10,... | collective-permute-start | bytes 196616 | tf_op jit(solution)/shard_map/ppermute | solution.py:363
  107.9 5.2 %collective-permute-start.8 = (f32[4,32,128]{2,1,0:T(8,128)S(1)}, f32[4,32,128]{2,1,0:T(8,128)S(1)}, u32[]{:S(2)}, u32[]{:S(2)}) collective-permute-start(f32[4,32,128]{2,1,0:T(8,128)S(1)} %add.42), channel_id=1, source_target_pairs={{0,6},{1,7},{2,4},{3,5},{4,2},{5,3},{6,0},{7,1},{8,14},{9,15},{10,... | collective-permute-start | bytes 196616 | tf_op jit(solution)/shard_map/ppermute | solution.py:363
  113.1 5.5 %collective-permute-start.10 = (f32[4,32,128]{2,1,0:T(8,128)S(1)}, f32[4,32,128]{2,1,0:T(8,128)S(1)}, u32[]{:S(2)}, u32[]{:S(2)}) collective-permute-start(f32[4,32,128]{2,1,0:T(8,128)S(1)} %add_add_fusion.3), channel_id=1, source_target_pairs={{0,16},{1,17},{2,18},{3,19},{4,20},{5,21},{6,22},{7,23},{8,24},{9,... | collective-permute-start | bytes 196616 | tf_op jit(solution)/shard_map/ppermute | solution.py:363
  116.2 6.2 %collective-permute-start.11 = (f32[4,32,128]{2,1,0:T(8,128)S(1)}, f32[4,32,128]{2,1,0:T(8,128)S(1)}, u32[]{:S(2)}, u32[]{:S(2)}) collective-permute-start(f32[4,32,128]{2,1,0:T(8,128)S(1)} %add_add_fusion.3), channel_id=1, source_target_pairs={{0,24},{1,25},{2,26},{3,27},{4,28},{5,29},{6,30},{7,31},{8,16},{9,... | collective-permute-start | bytes 196616 | tf_op jit(solution)/shard_map/ppermute | solution.py:363
  117.6 5.0 %collective-permute-start.9 = (f32[4,32,128]{2,1,0:T(8,128)S(1)}, f32[4,32,128]{2,1,0:T(8,128)S(1)}, u32[]{:S(2)}, u32[]{:S(2)}) collective-permute-start(f32[4,32,128]{2,1,0:T(8,128)S(1)} %add_add_fusion.3), channel_id=1, source_target_pairs={{0,8},{1,9},{2,10},{3,11},{4,12},{5,13},{6,14},{7,15},{8,0},{9,1},... | collective-permute-start | bytes 196616 | tf_op jit(solution)/shard_map/ppermute | solution.py:363
  122.6 1.3 collective-permute-start.12
  124.4 1.3 collective-permute-start.13
  125.7 4.4 %collective-permute-start.14 = (f32[4,32,128]{2,1,0:T(8,128)S(1)}, f32[4,32,128]{2,1,0:T(8,128)S(1)}, u32[]{:S(2)}, u32[]{:S(2)}) collective-permute-start(f32[4,32,128]{2,1,0:T(8,128)S(1)} %add.49), channel_id=1, source_target_pairs={{0,2},{1,3},{2,0},{3,1},{4,6},{5,7},{6,4},{7,5},{8,10},{9,11},{10,... | collective-permute-start | bytes 196616 | tf_op jit(solution)/shard_map/ppermute | solution.py:363
  126.3 5.0 %collective-permute-start.15 = (f32[4,32,128]{2,1,0:T(8,128)S(1)}, f32[4,32,128]{2,1,0:T(8,128)S(1)}, u32[]{:S(2)}, u32[]{:S(2)}) collective-permute-start(f32[4,32,128]{2,1,0:T(8,128)S(1)} %add.49), channel_id=1, source_target_pairs={{0,4},{1,5},{2,6},{3,7},{4,0},{5,1},{6,2},{7,3},{8,12},{9,13},{10,... | collective-permute-start | bytes 196616 | tf_op jit(solution)/shard_map/ppermute | solution.py:363
  126.8 5.2 %collective-permute-start.16 = (f32[4,32,128]{2,1,0:T(8,128)S(1)}, f32[4,32,128]{2,1,0:T(8,128)S(1)}, u32[]{:S(2)}, u32[]{:S(2)}) collective-permute-start(f32[4,32,128]{2,1,0:T(8,128)S(1)} %add.49), channel_id=1, source_target_pairs={{0,6},{1,7},{2,4},{3,5},{4,2},{5,3},{6,0},{7,1},{8,14},{9,15},{10,... | collective-permute-start | bytes 196616 | tf_op jit(solution)/shard_map/ppermute | solution.py:363
  132.0 4.5 %collective-permute-start.17 = (f32[4,32,128]{2,1,0:T(8,128)S(1)}, f32[4,32,128]{2,1,0:T(8,128)S(1)}, u32[]{:S(2)}, u32[]{:S(2)}) collective-permute-start(f32[4,32,128]{2,1,0:T(8,128)S(1)} %add_add_fusion.1), channel_id=1, source_target_pairs={{0,8},{1,9},{2,10},{3,11},{4,12},{5,13},{6,14},{7,15},{8,0},{9,1},... | collective-permute-start | bytes 196616 | tf_op jit(solution)/shard_map/ppermute | solution.py:363
  132.1 6.6 %collective-permute-start.18 = (f32[4,32,128]{2,1,0:T(8,128)S(1)}, f32[4,32,128]{2,1,0:T(8,128)S(1)}, u32[]{:S(2)}, u32[]{:S(2)}) collective-permute-start(f32[4,32,128]{2,1,0:T(8,128)S(1)} %add_add_fusion.1), channel_id=1, source_target_pairs={{0,16},{1,17},{2,18},{3,19},{4,20},{5,21},{6,22},{7,23},{8,24},{9,... | collective-permute-start | bytes 196616 | tf_op jit(solution)/shard_map/ppermute | solution.py:363
  134.4 6.1 %collective-permute-start.19 = (f32[4,32,128]{2,1,0:T(8,128)S(1)}, f32[4,32,128]{2,1,0:T(8,128)S(1)}, u32[]{:S(2)}, u32[]{:S(2)}) collective-permute-start(f32[4,32,128]{2,1,0:T(8,128)S(1)} %add_add_fusion.1), channel_id=1, source_target_pairs={{0,24},{1,25},{2,26},{3,27},{4,28},{5,29},{6,30},{7,31},{8,16},{9,... | collective-permute-start | bytes 196616 | tf_op jit(solution)/shard_map/ppermute | solution.py:363
  140.5 2.2 %collective-permute-start.20 = (f32[4,32,128]{2,1,0:T(8,128)S(1)}, f32[4,32,128]{2,1,0:T(8,128)S(1)}, u32[]{:S(2)}, u32[]{:S(2)}) collective-permute-start(f32[4,32,128]{2,1,0:T(8,128)S(1)} %add_add_fusion.mine_ref), channel_id=1, source_target_pairs={{0,1},{1,0},{2,3},{3,2},{4,5},{5,4},{6,7},{7,6},{8,9},{9,8},{10,11... | collective-permute-start | bytes 196616 | tf_op jit(solution)/shard_map/ppermute | solution.py:347

commit v2 on v1

v2 whole, which is shorter than its diff:
```python
import functools
import itertools

import jax
import jax.numpy as jnp
from jax import lax
from jax.experimental import pallas as pl
from jax.experimental.pallas import tpu as pltpu
from jax.sharding import PartitionSpec as P


HIGHEST = lax.Precision.HIGHEST
VMEM = pl.BlockSpec(memory_space=pltpu.VMEM)
ANY = pl.BlockSpec(memory_space=pl.ANY)
ELIMINATE = 8
PROJECT = 512


def params(mib):
    return pltpu.CompilerParams(vmem_limit_bytes=mib << 20)


def f32(*shape):
    return jax.ShapeDtypeStruct(shape, jnp.float32)


def bf16(*shape):
    return jax.ShapeDtypeStruct(shape, jnp.bfloat16)


def dot(a, b, contract, precision=None):
    return lax.dot_general(
        a, b, (contract, ((), ())), precision=precision, preferred_element_type=jnp.float32
    )


NN = ((1,), (0,))
NT = ((1,), (1,))


def halves(value):
    high = value.astype(jnp.bfloat16)
    return high, (value - high.astype(jnp.float32)).astype(jnp.bfloat16)


def dot3(a, b, contract):
    return dot(a[0], b[0], contract) + (dot(a[0], b[1], contract) + dot(a[1], b[0], contract))


def eye(n):
    return jnp.where(
        lax.broadcasted_iota(jnp.int32, (n, n), 0) == lax.broadcasted_iota(jnp.int32, (n, n), 1), 1.0, 0.0
    ).astype(jnp.float32)


def inverse_factor(squares):
    n = squares.shape[0]
    wide = 2 * n
    step = ELIMINATE
    start = jnp.concatenate([squares, eye(n)], axis=1)
    rows = [start[i : i + step] for i in range(0, n, step)]
    below = lax.broadcasted_iota(jnp.int32, (step, wide), 0)
    for t in range(n // step):
        columns = [
            {i: jnp.broadcast_to(rows[i][:, t * step + j : t * step + j + 1], (step, wide)) for i in range(t, n // step)}
            for j in range(step)
        ]
        pivots = [rows[t][j : j + 1, :] for j in range(step)]
        update = {}
        for j in range(step):
            inverse = 1.0 / columns[j][t][j : j + 1, :]
            scaled = {i: columns[j][i] * inverse for i in range(t, n // step)}
            scaled[t] = jnp.where(below > j, scaled[t], 0.0)
            for i in range(t, n // step):
                term = scaled[i] * pivots[j]
                update[i] = update[i] + term if i in update else term
            for m in range(j + 1, step):
                pivots[m] = pivots[m] - scaled[t][m : m + 1, :] * pivots[j]
                across = columns[m][t][j : j + 1, :]
                for i in range(t, n // step):
                    columns[m][i] = columns[m][i] - scaled[i] * across
        for i in range(t, n // step):
            rows[i] = rows[i] - update[i]
    done = jnp.concatenate(rows, axis=0)
    left, right = done[:, :n], done[:, n:]
    diagonal = jnp.sum(left * eye(n), axis=1, keepdims=True)
    return right * lax.rsqrt(diagonal)


def extract_kernel(shift, row, tensor_ref, out_ref, sem):
    rows = out_ref.shape[0]
    which = lax.axis_index("fibre") ^ shift
    copy = pltpu.make_async_copy(tensor_ref.at[pl.ds(row, rows), 0, which, :], out_ref, sem)
    copy.start()
    copy.wait()


def extract(shift, tensor, row, rows):
    width = tensor.shape[3]
    return pl.pallas_call(
        functools.partial(extract_kernel, shift, row),
        out_shape=f32(rows, width),
        in_specs=[ANY],
        out_specs=VMEM,
        scratch_shapes=[pltpu.SemaphoreType.DMA(())],
        compiler_params=params(62),
        cost_estimate=pl.CostEstimate(flops=0, bytes_accessed=8 * rows * width, transcendentals=0),
        name="extract",
    )(tensor)


def cross(every, new):
    size, rows = every[0].shape[0], new[0].shape[0]
    full = dot(jnp.concatenate(every, axis=0), jnp.concatenate(new, axis=0), NT)
    return full[:size, :rows] + (full[:size, rows:] + full[size:, :rows] + full[size:, rows:])


def joined(refs):
    return [jnp.concatenate([ref[...] for ref in refs[s::2]], axis=0) for s in range(2)]


def low_core():
    return lax.axis_index("cols") % 2 == 0


def shares(value):
    half = value.shape[0] // 2
    low, high = value[:half], value[half:]
    return jnp.where(low_core(), low, high), jnp.where(low_core(), high, low)


def merged(mine, other):
    return jnp.concatenate([jnp.where(low_core(), mine, other), jnp.where(low_core(), other, mine)], axis=0)


def in_turn(ref, shifts):
    me = lax.axis_index("fibre")
    return jnp.concatenate([ref[me ^ shift] for shift in shifts], axis=1)


def by_fibre(ref):
    return jnp.concatenate([ref[f] for f in range(ref.shape[0])], axis=1)


def put(value, shifts, ref):
    me, rows = lax.axis_index("fibre"), ref.shape[2]
    for p, shift in enumerate(shifts):
        ref[me ^ shift] = value[:, p * rows : (p + 1) * rows]


def arrive_kernel(parts, before, share, *refs):
    piece = jnp.concatenate([ref[...] for ref in refs[:parts]], axis=0)
    old = refs[parts : parts + 2 * before]
    state = refs[parts + 2 * before : parts + 2 * before + bool(before)]
    high_ref, low_ref, *gram_refs = refs[parts + 2 * before + bool(before) :]
    new = halves(piece)
    high_ref[...], low_ref[...] = new
    if before:
        column = cross([jnp.concatenate(pair, axis=0) for pair in zip(joined(old), new)], new)
        side = state[0].shape[0]
        gram = jnp.concatenate([jnp.concatenate([state[0][...], column[:side].T], axis=0), column], axis=1)
    else:
        gram = cross(new, new)
    for ref, value in zip(gram_refs, shares(gram) if share else [gram]):
        ref[...] = value


def arrive(parts, old, state, share):
    rows, width = sum(part.shape[0] for part in parts), parts[0].shape[1]
    size = sum(piece.shape[0] for piece in old[::2]) + rows
    out = (bf16(rows, width),) * 2 + ((f32(size // 2, size),) * 2 if share else (f32(size, size),))
    return pl.pallas_call(
        functools.partial(arrive_kernel, len(parts), len(old) // 2, share),
        out_shape=out,
        in_specs=[VMEM] * (len(parts) + len(old) + len(state)),
        out_specs=(VMEM,) * len(out),
        compiler_params=params(24),
        cost_estimate=pl.CostEstimate(
            flops=8 * rows * width * size, bytes_accessed=4 * width * size, transcendentals=0
        ),
        name="arrive",
    )(*parts, *old, *state)


def stripe_kernel(piece_ref, *refs):
    old, (high_ref, low_ref, mine_ref, other_ref) = refs[:-4], refs[-4:]
    new = halves(piece_ref[...])
    high_ref[...], low_ref[...] = new
    column = cross([jnp.concatenate(pair, axis=0) for pair in zip(joined(old), new)], new)
    mine_ref[...], other_ref[...] = shares(column.T)


def stripe(part, old):
    rows, width = part.shape
    size = sum(piece.shape[0] for piece in old[::2]) + rows
    return pl.pallas_call(
        stripe_kernel,
        out_shape=(bf16(rows, width),) * 2 + (f32(rows // 2, size),) * 2,
        in_specs=[VMEM] * (1 + len(old)),
        out_specs=(VMEM,) * 4,
        compiler_params=params(24),
        cost_estimate=pl.CostEstimate(
            flops=8 * rows * width * size, bytes_accessed=4 * width * size, transcendentals=0
        ),
        name="stripe",
    )(part, *old)


def ranks_here(basis):
    half = basis.shape[0] // 2
    return jnp.where(low_core(), basis[:half], basis[half:])


def assemble_kernel(shifts, basis_ref, gram_mine, gram_other, mine_ref, other_ref, high_ref, low_ref, image_ref):
    block = merged(gram_mine[...], gram_other[...])
    lower = merged(mine_ref[...], other_ref[...])
    side = block.shape[0]
    gram = jnp.concatenate(
        [jnp.concatenate([block, lower[:, :side]], axis=0), lower.T], axis=1
    )
    split = halves(gram)
    high_ref[...], low_ref[...] = split
    basis = halves(ranks_here(in_turn(basis_ref, shifts))[:, : gram.shape[0]])
    image_ref[...] = dot3(basis, split, NN)


def assemble(shifts, basis, block, lower):
    size = lower[0].shape[1]
    return pl.pallas_call(
        functools.partial(assemble_kernel, shifts),
        out_shape=(bf16(size, size), bf16(size, size), f32(basis.shape[1] // 2, size)),
        in_specs=[VMEM] * 5,
        out_specs=(VMEM,) * 3,
        compiler_params=params(16),
        name="assemble",
    )(basis, *block, *lower)


def with_stripe(early, image, stripe):
    side = stripe[0].shape[1] - stripe[0].shape[0]
    late = dot3(image, stripe, NT)
    early = early + dot3([v[:, side:] for v in image], [v[:, :side] for v in stripe], NN)
    return jnp.concatenate([early, late], axis=1)


def first_kernel(shifts, basis_ref, image_ref, mine_ref, other_ref, out_ref):
    basis = halves(ranks_here(in_turn(basis_ref, shifts)))
    put(with_stripe(image_ref[...], basis, halves(merged(mine_ref[...], other_ref[...]))), shifts, out_ref)


def first(shifts, basis, image, stripe):
    fibres, ranks, rows = basis.shape
    return pl.pallas_call(
        functools.partial(first_kernel, shifts),
        out_shape=f32(fibres, ranks // 2, rows),
        in_specs=[VMEM] * 4,
        out_specs=VMEM,
        compiler_params=params(16),
        name="first",
    )(basis, image, *stripe)


def second_kernel(shifts, image_ref, high_ref, low_ref, mine_ref, other_ref, out_ref):
    image = halves(in_turn(image_ref, shifts))
    side = high_ref.shape[0]
    early = dot3([v[:, :side] for v in image], (high_ref[...], low_ref[...]), NN)
    put(with_stripe(early, image, halves(merged(mine_ref[...], other_ref[...]))), shifts, out_ref)


def second(shifts, image, gram, stripe):
    return pl.pallas_call(
        functools.partial(second_kernel, shifts),
        out_shape=f32(*image.shape),
        in_specs=[VMEM] * 5,
        out_specs=VMEM,
        compiler_params=params(16),
        name="second",
    )(image, *gram, *stripe)


def factor_kernel(mine_ref, other_ref, out_ref):
    image = merged(by_fibre(mine_ref), by_fibre(other_ref))
    out_ref[...] = inverse_factor(dot(image, image, NT, HIGHEST))


def factor(mine, other):
    ranks = 2 * mine.shape[1]
    return pl.pallas_call(
        factor_kernel,
        out_shape=f32(ranks, ranks),
        in_specs=[VMEM] * 2,
        out_specs=VMEM,
        compiler_params=params(8),
        cost_estimate=pl.CostEstimate(flops=40 * ranks**3, bytes_accessed=8 * mine.size, transcendentals=0),
        name="factor",
    )(mine, other)


def close_kernel(shifts, mine_ref, other_ref, inverse_ref, *refs):
    pieces, (core_ref, basis_ref, slab, sems) = refs[:-4], refs[-4:]
    first = inverse_ref[...]
    image = dot(first, merged(by_fibre(mine_ref), by_fibre(other_ref)), NN, HIGHEST)
    turned = dot(first, merged(in_turn(mine_ref, shifts), in_turn(other_ref, shifts)), NN, HIGHEST)
    parts = halves(turned)
    inverse = inverse_factor(dot(image, image, NT, HIGHEST))
    width = core_ref.shape[3]
    chunk = min(PROJECT, width)
    raw = []
    for c in range(0, width, chunk):
        columns = [jnp.concatenate([ref[:, c : c + chunk] for ref in pieces[k::2]], axis=0) for k in range(2)]
        raw.append(dot3(parts, columns, NN))
    basis_ref[...] = dot(inverse, image, NN, HIGHEST)
    split = halves(inverse)
    stores = []
    for n, c in enumerate(range(0, width, chunk)):
        slab[:, c : c + chunk] = dot3(split, halves(raw[n]), NN)
        stores.append(
            pltpu.make_async_copy(slab.at[:, pl.ds(c, chunk)], core_ref.at[:, 0, 0, pl.ds(c, chunk)], sems.at[n])
        )
        stores[-1].start()
    for store in stores:
        store.wait()


def close(shifts, mine, other, inverse, pieces):
    fibres, half, rows = mine.shape
    width = pieces[0].shape[1]
    return pl.pallas_call(
        functools.partial(close_kernel, shifts),
        out_shape=(f32(2 * half, 1, 1, width), f32(2 * half, fibres * rows)),
        in_specs=[VMEM] * (3 + len(pieces)),
        out_specs=(ANY, VMEM),
        scratch_shapes=[
            pltpu.VMEM((2 * half, width), jnp.float32),
            pltpu.SemaphoreType.DMA((width // min(PROJECT, width),)),
        ],
        compiler_params=params(24),
        name="close",
    )(mine, other, inverse, *pieces)


def swap(value, axis, size, bit):
    return lax.ppermute(value, axis, [(i, i ^ bit) for i in range(size)])


def bits(size):
    return [1 << b for b in range(size.bit_length() - 1)]


def crossings(flips):
    return [flips[i : i + 2] for i in range(0, len(flips), 2)]


def over_chips(value, axis, size):
    for flips in crossings(bits(size)[axis == "cols" :]):
        if len(flips) == 1:
            value = value + swap(value, axis, size, flips[0])
            continue
        one, two, three = (swap(value, axis, size, flip) for flip in (*flips, flips[0] ^ flips[1]))
        value = (value + one) + (two + three)
    return value


def over_cols(mine, other, n_cols):
    mine = over_chips(mine + swap(other, "cols", n_cols, 1), "cols", n_cols)
    return mine, swap(mine, "cols", n_cols, 1)


def turns(n_fibre):
    images = [n_fibre - 1] + bits(n_fibre)[:-1]
    out = []
    for p in range(n_fibre):
        shift = 0
        for b, image in enumerate(images):
            shift ^= image if p >> b & 1 else 0
        out.append(shift)
    return out


def shards(n_fibre, n_cols, tensor, initial):
    rows = tensor.shape[0]
    shifts = turns(n_fibre)
    start = initial.reshape(n_fibre, rows, initial.shape[1]).transpose(0, 2, 1)

    last = n_fibre - 1
    cuts = {1: (0, rows // 2, rows), last: (0, rows // 2, rows)}
    parts, sends = {}, 0
    for p in [*range(1, last), 0, last]:
        parts[p] = []
        for row, end in itertools.pairwise(cuts.get(p, (0, rows))):
            part = extract(shifts[p], tensor, row, end - row)
            if p:
                part = swap(part, "fibre", n_fibre, shifts[p])
                sends += 1
            parts[p].append(part)

    pieces, state = (), ()
    for p in range(last):
        high, low, *state = arrive(parts[p], pieces, state, p == last - 1)
        pieces += (high, low)
    block = over_cols(*state, n_cols)
    high, low, *lower = stripe(parts[last][0], pieces)
    pieces += (high, low)
    lower = over_cols(*lower, n_cols)
    *gram, image = assemble(shifts, start, block, lower)
    high, low, *lower = stripe(parts[last][1], pieces)
    pieces += (high, low)
    lower = over_cols(*lower, n_cols)

    mine = over_chips(first(shifts, start, image, lower), "fibre", n_fibre)
    other = swap(mine, "cols", n_cols, 1)
    inverse = factor(mine, other)
    mine = second(shifts, mine, gram, lower)
    mine = over_chips(mine, "fibre", n_fibre)
    core_slab, basis_t = close(shifts, mine, swap(mine, "cols", n_cols, 1), inverse, pieces)
    return (core_slab, basis_t.T)


def solution(mesh):
    n_fibre, n_cols = mesh.shape["fibre"], mesh.shape["cols"]
    placed = (P("fibre", "cols", None, None), P())

    def body(tensor, initial):
        return shards(n_fibre, n_cols, tensor, initial)

    return jax.shard_map(
        body,
        mesh=mesh,
        in_specs=placed,
        out_specs=(P(None, "cols", "fibre", None), P()),
        check_vma=False,
    )
```

time: 148 us -> 159 us (1.074)
  waiting for transfers between devices: 91.3 us -> 99.6 us
  starting transfers between devices: 26.3 us -> 28.8 us
    ppermute x9 -> x28, waiting for transfers between devices: 74.8 us -> 99.6 us  [swap(): return lax.ppermute(value, axis, [(i, i ^ bit) for i in range(size)])]
    ppermute x9 -> x28, starting transfers between devices: 10.2 us -> 28.8 us  [swap(): return lax.ppermute(value, axis, [(i, i ^ bit) for i in range(size)])]
    ppermute x12 -> x0, waiting for transfers between devices: 16.4 us -> none  [across(): return lax.ppermute(value, ('fibre', 'cols'), perm)]
    ppermute x12 -> x0, starting transfers between devices: 16.1 us -> none  [across(): return lax.ppermute(value, ('fibre', 'cols'), perm)]
    pallas_call x13 -> x15, Pallas kernels: 25.5 us -> 25.2 us  [the longest x6 12 us: extract(): pl.pallas_call(functools.partial(extract_kernel, shift, row), out_shape=f...]
  transfers between devices with their start and end apart: 21 -> 28, of which waited for: 17 -> 13; matrix products, arithmetic and copies ran while one was open for 0% -> 0% of each run, Pallas kernels for 12% -> 13%
where the time goes in v2:
time: 159 us; the launch traced here: 158 us
  waiting for transfers between devices  99.6 us (63%)
  starting transfers between devices  28.8 us (18%)
  Pallas kernels  27.4 us (17%)
    ppermute x28, waiting for transfers between devices, swap(): return lax.ppermute(value, axis, [(i, i ^ bit) for i in range(size)])  99.6 us
    ppermute x28, starting transfers between devices, swap(): return lax.ppermute(value, axis, [(i, i ^ bit) for i in range(size)])  28.8 us
    pallas_call x6, Pallas kernels, extract(): pl.pallas_call(functools.partial(extract_kernel, shift, row), out_shape=f...  12 us
    pallas_call x1, Pallas kernels, close(): pl.pallas_call(functools.partial(close_kernel, shifts), out_shape=(f32(2...  4.59 us
    pallas_call x2, Pallas kernels, stripe(): pl.pallas_call(stripe_kernel, out_shape=(bf16(rows, width),) * 2 + (f32(r...  3.89 us
    pallas_call x3, Pallas kernels, arrive(): pl.pallas_call(functools.partial(arrive_kernel, len(parts), len(old) // 2...  3.62 us
  transfers between devices with their start and end apart: 28, of which 13 were waited for; matrix products, arithmetic and copies ran while one was open for 0% of the time, Pallas kernels for 13%

profile of v2, /device:TPU:0, one launch (start us, length us, event | category | flops | bytes accessed | tf_op | source)
XLA Modules:
  0.0 158.1 jit_solution(7883001171285465629)
XLA Ops:
  0.6 0.0 copy-start
  0.6 2.3 %extract.6 = f32[128,2048]{1,0:T(8,128)} custom-call(f32[128,1,4,2048]{3,2,1,0:T(4,128)} %tensor_ref.11), custom_call_target="tpu_custom_call" | custom-call | bytes 2097152 | tf_op jit(solution)/shard_map/extract/pallas_call | solution.py:100
  2.9 3.1 %collective-permute-start = (f32[128,2048]{1,0:T(8,128)}, f32[128,2048]{1,0:T(8,128)S(1)}, u32[]{:S(2)}, u32[]{:S(2)}) collective-permute-start(f32[128,2048]{1,0:T(8,128)} %extract.6), channel_id=1, source_target_pairs={{0,8},{8,0},{16,24},{24,16},{1,9},{9,1},{17,25},{25,17},{2,10},{10... | collective-permute-start | bytes 3145736 | tf_op jit(solution)/shard_map/ppermute | solution.py:343
  6.1 1.9 %extract.8 = f32[64,2048]{1,0:T(8,128)} custom-call(f32[128,1,4,2048]{3,2,1,0:T(4,128)} %tensor_ref.11), custom_call_target="tpu_custom_call" | custom-call | bytes 1048576 | tf_op jit(solution)/shard_map/extract/pallas_call | solution.py:100
  7.9 2.5 %collective-permute-start.1 = (f32[64,2048]{1,0:T(8,128)}, f32[64,2048]{1,0:T(8,128)}, u32[]{:S(2)}, u32[]{:S(2)}) collective-permute-start(f32[64,2048]{1,0:T(8,128)} %extract.8), channel_id=1, source_target_pairs={{0,24},{8,16},{16,8},{24,0},{1,25},{9,17},{17,9},{25,1},{2,26},{10... | collective-permute-start | bytes 1572872 | tf_op jit(solution)/shard_map/ppermute | solution.py:343
  10.5 1.9 %extract.9 = f32[64,2048]{1,0:T(8,128)} custom-call(f32[128,1,4,2048]{3,2,1,0:T(4,128)} %tensor_ref.11), custom_call_target="tpu_custom_call" | custom-call | bytes 1048576 | tf_op jit(solution)/shard_map/extract/pallas_call | solution.py:100
  12.4 1.4 collective-permute-start.2
  13.8 1.9 %extract.10 = f32[64,2048]{1,0:T(8,128)} custom-call(f32[128,1,4,2048]{3,2,1,0:T(4,128)} %tensor_ref.11), custom_call_target="tpu_custom_call" | custom-call | bytes 1048576 | tf_op jit(solution)/shard_map/extract/pallas_call | solution.py:100
  15.7 0.9 collective-permute-start.8
  16.5 1.9 %extract.11 = f32[64,2048]{1,0:T(8,128)} custom-call(f32[128,1,4,2048]{3,2,1,0:T(4,128)} %tensor_ref.11), custom_call_target="tpu_custom_call" | custom-call | bytes 1048576 | tf_op jit(solution)/shard_map/extract/pallas_call | solution.py:100
  18.4 2.2 %collective-permute-start.14 = (f32[64,2048]{1,0:T(8,128)}, f32[64,2048]{1,0:T(8,128)}, u32[]{:S(2)}, u32[]{:S(2)}) collective-permute-start(f32[64,2048]{1,0:T(8,128)} %extract.11), channel_id=1, source_target_pairs={{0,16},{8,24},{16,0},{24,8},{1,17},{9,25},{17,1},{25,9},{2,18},{10... | collective-permute-start | bytes 1572872 | tf_op jit(solution)/shard_map/ppermute | solution.py:343
  20.6 2.2 %extract.7.refs_0_ = f32[128,2048]{1,0:T(8,128)} custom-call(f32[128,1,4,2048]{3,2,1,0:T(4,128)} %tensor_ref.11), custom_call_target="tpu_custom_call" | custom-call | bytes 2097152 | tf_op jit(solution)/shard_map/extract/pallas_call | solution.py:100
  22.8 1.2 copy-done.1
  24.1 0.5 arrive.3
  24.6 19.6 %collective-permute-done.1.refs_0_ = f32[64,2048]{1,0:T(8,128)} collective-permute-done((f32[64,2048]{1,0:T(8,128)}, f32[64,2048]{1,0:T(8,128)}, u32[]{:S(2)}, u32[]{:S(2)}) %collective-permute-start.1) | collective-permute-done | bytes 524320 | tf_op jit(solution)/shard_map/ppermute | solution.py:343
  44.2 11.2 %collective-permute-done.2.refs_1_ = f32[64,2048]{1,0:T(8,128)} collective-permute-done((f32[64,2048]{1,0:T(8,128)}, f32[64,2048]{1,0:T(8,128)}, u32[]{:S(2)}, u32[]{:S(2)}) %collective-permute-start.2) | collective-permute-done | bytes 524320 | tf_op jit(solution)/shard_map/ppermute | solution.py:343
  55.4 2.0 %arrive.4 = (bf16[128,2048]{1,0:T(8,128)(2,1)S(1)}, bf16[128,2048]{1,0:T(8,128)(2,1)S(1)}, f32[256,256]{1,0:T(8,128)S(1)}) custom-call(f32[64,2048]{1,0:T(8,128)} %collective-permute-done.1.refs_0_, f32[64,2048]{1,0:T(8,128)} %collective-permute-done.2.refs_1_, bf16[128,2048]{1,0:T(8,128)(2,1)S(1)} %get-tuple-element.25.refs_2_.refs_1_.refs_0_, ...), custom_call_target="tpu_custom_call" | custom-call | flops 536870912 | bytes 2097152 | tf_op jit(solution)/shard_map/arrive/pallas_call | solution.py:172
  57.4 1.1 arrive.5
  58.5 0.1 collective-permute-start.3
  58.6 32.4 %collective-permute-done.8.piece_ref = f32[64,2048]{1,0:T(8,128)S(1)} collective-permute-done((f32[64,2048]{1,0:T(8,128)}, f32[64,2048]{1,0:T(8,128)S(1)}, u32[]{:S(2)}, u32[]{:S(2)}) %collective-permute-start.8) | collective-permute-done | bytes 524320 | tf_op jit(solution)/shard_map/ppermute | solution.py:343
  91.0 1.4 stripe.2
  92.4 0.1 collective-permute-start.9
  92.4 8.8 %collective-permute-done.14.piece_ref = f32[64,2048]{1,0:T(8,128)} collective-permute-done((f32[64,2048]{1,0:T(8,128)}, f32[64,2048]{1,0:T(8,128)}, u32[]{:S(2)}, u32[]{:S(2)}) %collective-permute-start.14) | collective-permute-done | bytes 524320 | tf_op jit(solution)/shard_map/ppermute | solution.py:343
  101.2 2.5 %stripe.3 = (bf16[64,2048]{1,0:T(8,128)(2,1)S(1)}, bf16[64,2048]{1,0:T(8,128)(2,1)S(1)}, f32[32,512]{1,0:T(8,128)S(1)}, f32[32,512]{1,0:T(8,128)S(1)}) custom-call(f32[64,2048]{1,0:T(8,128)} %collective-permute-done.14.piece_ref, bf16[128,2048]{1,0:T(8,128)(2,1)S(1)} %get-tuple-element.25.refs_2_.refs_1_.refs_0_, ...), custom_call_target="tpu_custom_call" | custom-call | flops 536870912 | bytes 4194304 | tf_op jit(solution)/shard_map/stripe/pallas_call | solution.py:196
  103.7 0.1 collective-permute-start.15
  103.8 0.0 collective-permute-done.9
  103.8 1.6 %collective-permute-start.11 = (f32[32,448]{1,0:T(8,128)S(1)}, f32[32,448]{1,0:T(8,128)S(1)}, u32[]{:S(2)}, u32[]{:S(2)}) collective-permute-start(f32[32,448]{1,0:T(8,128)S(1)} %add.58), channel_id=1, source_target_pairs={{0,4},{1,5},{2,6},{3,7},{4,0},{5,1},{6,2},{7,3},{8,12},{9,13},{10,... | collective-permute-start | bytes 172040 | tf_op jit(solution)/shard_map/ppermute | solution.py:343
  105.4 0.0 collective-permute-done.3
  105.5 0.6 collective-permute-start.5
  106.0 2.4 %collective-permute-start.6 = (f32[192,384]{1,0:T(8,128)S(1)}, f32[192,384]{1,0:T(8,128)S(1)}, u32[]{:S(2)}, u32[]{:S(2)}) collective-permute-start(f32[192,384]{1,0:T(8,128)S(1)} %add.54), channel_id=1, source_target_pairs={{0,6},{1,7},{2,4},{3,5},{4,2},{5,3},{6,0},{7,1},{8,14},{9,15},{10,... | collective-permute-start | bytes 884744 | tf_op jit(solution)/shard_map/ppermute | solution.py:343
  108.5 0.5 collective-permute-start.4
  109.0 1.4 collective-permute-start.12
  110.5 0.5 collective-permute-start.10
  111.0 13.2 %collective-permute-done.12 = f32[32,448]{1,0:T(8,128)S(1)} collective-permute-done((f32[32,448]{1,0:T(8,128)S(1)}, f32[32,448]{1,0:T(8,128)S(1)}, u32[]{:S(2)}, u32[]{:S(2)}) %collective-permute-start.12) | collective-permute-done | bytes 57376 | tf_op jit(solution)/shard_map/ppermute | solution.py:343
  124.3 1.5 collective-permute-start.17
  125.8 1.4 collective-permute-start.18
  127.2 0.0 collective-permute-done.5
  127.2 0.6 collective-permute-start.16
  127.9 0.0 collective-permute-start.13
  127.9 0.0 collective-permute-done.4
  127.9 0.1 add_add_fusion.gram_mine
  127.9 0.6 collective-permute-start.7
  128.5 0.5 collective-permute-done.17
  129.0 1.9 %collective-permute-done.18 = f32[32,512]{1,0:T(8,128)S(1)} collective-permute-done((f32[32,512]{1,0:T(8,128)S(1)}, f32[32,512]{1,0:T(8,128)S(1)}, u32[]{:S(2)}, u32[]{:S(2)}) %collective-permute-start.18) | collective-permute-done | bytes 65568 | tf_op jit(solution)/shard_map/ppermute | solution.py:343
  130.9 0.6 collective-permute-done.16
  131.6 0.1 collective-permute-start.19
  131.7 0.0 collective-permute-done.13.other_ref
  131.7 0.5 assemble.1
  132.2 0.7 collective-permute-done.19.other_ref
  132.9 0.3 first.1
  133.2 0.0 collective-permute-start.21
  133.3 2.7 %collective-permute-start.22 = (f32[4,32,128]{2,1,0:T(8,128)S(1)}, f32[4,32,128]{2,1,0:T(8,128)S(1)}, u32[]{:S(2)}, u32[]{:S(2)}) collective-permute-start(f32[4,32,128]{2,1,0:T(8,128)S(1)} %first.1), channel_id=1, source_target_pairs={{0,24},{8,16},{16,8},{24,0},{1,25},{9,17},{17,9},{25,1},{2,26},{10... | collective-permute-start | bytes 196616 | tf_op jit(solution)/shard_map/ppermute | solution.py:343
  136.0 0.8 collective-permute-start.20
  136.7 4.5 %collective-permute-done.21 = f32[4,32,128]{2,1,0:T(8,128)S(1)} collective-permute-done((f32[4,32,128]{2,1,0:T(8,128)S(1)}, f32[4,32,128]{2,1,0:T(8,128)S(1)}, u32[]{:S(2)}, u32[]{:S(2)}) %collective-permute-start.21) | collective-permute-done | bytes 65568 | tf_op jit(solution)/shard_map/ppermute | solution.py:343
  141.2 1.1 collective-permute-done.20
  142.3 0.4 second.1
  142.8 0.6 collective-permute-start.24
  143.4 2.6 %collective-permute-start.25 = (f32[4,32,128]{2,1,0:T(8,128)S(1)}, f32[4,32,128]{2,1,0:T(8,128)S(1)}, u32[]{:S(2)}, u32[]{:S(2)}) collective-permute-start(f32[4,32,128]{2,1,0:T(8,128)S(1)} %second.1), channel_id=1, source_target_pairs={{0,24},{8,16},{16,8},{24,0},{1,25},{9,17},{17,9},{25,1},{2,26},{10... | collective-permute-start | bytes 196616 | tf_op jit(solution)/shard_map/ppermute | solution.py:343
  146.0 0.3 collective-permute-start.23
  146.3 4.6 %collective-permute-done.24 = f32[4,32,128]{2,1,0:T(8,128)S(1)} collective-permute-done((f32[4,32,128]{2,1,0:T(8,128)S(1)}, f32[4,32,128]{2,1,0:T(8,128)S(1)}, u32[]{:S(2)}, u32[]{:S(2)}) %collective-permute-start.24) | collective-permute-done | bytes 65568 | tf_op jit(solution)/shard_map/ppermute | solution.py:343
  150.9 0.4 collective-permute-done.23
  151.3 0.1 collective-permute-start.26
  151.4 2.1 %factor.1.inverse_ref = f32[64,64]{1,0:T(8,128)S(1)} custom-call(f32[4,32,128]{2,1,0:T(8,128)S(1)} %add_add_fusion.2.image_ref.mine_ref, f32[4,32,128]{2,1,0:T(8,128)S(1)} %collective-permute-done.27.other_ref), custom_call_target="tpu_custom_call" | custom-call | flops 10485760 | bytes 131072 | tf_op jit(solution)/shard_map/factor/pallas_call | solution.py:288
  153.5 4.6 %close.1 = (f32[64,1,1,2048]{3,2,1,0:T(1,128)}, f32[64,512]{1,0:T(8,128)}) custom-call(f32[4,32,128]{2,1,0:T(8,128)S(1)} %add_add_fusion.1.mine_ref, f32[4,32,128]{2,1,0:T(8,128)S(1)} %collective-permute-done.26.other_ref, f32[64,64]{1,0:T(8,128)S(1)} %factor.1.inverse_ref, bf16[128,2048]{1,0:T(8,128)(2,1)S(1)} %get-tuple-element.25.refs_2_.refs_1_.refs_0_, ...), custom_call_target="tpu_custom_call" | custom-call | tf_op jit(solution)/shard_map/close/pallas_call | solution.py:328
  (21 shorter events, 0.2 us)
Async XLA Ops:
  0.6 131.1 %copy-start = (f32[512,64]{0,1:T(8,128)S(1)}, f32[512,64]{0,1:T(8,128)}, u32[]{:S(2)}) copy-start(f32[512,64]{0,1:T(8,128)} %param.3) | copy-start | bytes 393220
  2.9 54.5 %collective-permute-start = (f32[128,2048]{1,0:T(8,128)}, f32[128,2048]{1,0:T(8,128)S(1)}, u32[]{:S(2)}, u32[]{:S(2)}) collective-permute-start(f32[128,2048]{1,0:T(8,128)} %extract.6), channel_id=1, source_target_pairs={{0,8},{8,0},{16,24},{24,16},{1,9},{9,1},{17,25},{25,17},{2,10},{10... | collective-permute-start | bytes 3145736 | tf_op jit(solution)/shard_map/ppermute | solution.py:343
  7.9 36.2 %collective-permute-start.1 = (f32[64,2048]{1,0:T(8,128)}, f32[64,2048]{1,0:T(8,128)}, u32[]{:S(2)}, u32[]{:S(2)}) collective-permute-start(f32[64,2048]{1,0:T(8,128)} %extract.8), channel_id=1, source_target_pairs={{0,24},{8,16},{16,8},{24,0},{1,25},{9,17},{17,9},{25,1},{2,26},{10... | collective-permute-start | bytes 1572872 | tf_op jit(solution)/shard_map/ppermute | solution.py:343
  12.4 43.0 %collective-permute-start.2 = (f32[64,2048]{1,0:T(8,128)}, f32[64,2048]{1,0:T(8,128)}, u32[]{:S(2)}, u32[]{:S(2)}) collective-permute-start(f32[64,2048]{1,0:T(8,128)} %extract.9), channel_id=1, source_target_pairs={{0,24},{8,16},{16,8},{24,0},{1,25},{9,17},{17,9},{25,1},{2,26},{10... | collective-permute-start | bytes 1572872 | tf_op jit(solution)/shard_map/ppermute | solution.py:343
  15.7 75.3 %collective-permute-start.8 = (f32[64,2048]{1,0:T(8,128)}, f32[64,2048]{1,0:T(8,128)S(1)}, u32[]{:S(2)}, u32[]{:S(2)}) collective-permute-start(f32[64,2048]{1,0:T(8,128)} %extract.10), channel_id=1, source_target_pairs={{0,16},{8,24},{16,0},{24,8},{1,17},{9,25},{17,1},{25,9},{2,18},{10... | collective-permute-start | bytes 1572872 | tf_op jit(solution)/shard_map/ppermute | solution.py:343
  18.4 82.8 %collective-permute-start.14 = (f32[64,2048]{1,0:T(8,128)}, f32[64,2048]{1,0:T(8,128)}, u32[]{:S(2)}, u32[]{:S(2)}) collective-permute-start(f32[64,2048]{1,0:T(8,128)} %extract.11), channel_id=1, source_target_pairs={{0,16},{8,24},{16,0},{24,8},{1,17},{9,25},{17,1},{25,9},{2,18},{10... | collective-permute-start | bytes 1572872 | tf_op jit(solution)/shard_map/ppermute | solution.py:343
  22.8 1.2 copy-start.1
  58.5 46.9 %collective-permute-start.3 = (f32[192,384]{1,0:T(8,128)S(1)}, f32[192,384]{1,0:T(8,128)S(1)}, u32[]{:S(2)}, u32[]{:S(2)}) collective-permute-start(f32[192,384]{1,0:T(8,128)S(1)} %get-tuple-element.32), channel_id=1, source_target_pairs={{0,1},{1,0},{2,3},{3,2},{4,5},{5,4},{6,7},{7,6},{8,9},{9,8},{10,11... | collective-permute-start | bytes 884744 | tf_op jit(solution)/shard_map/ppermute | solution.py:343
  92.4 11.5 %collective-permute-start.9 = (f32[32,448]{1,0:T(8,128)S(1)}, f32[32,448]{1,0:T(8,128)S(1)}, u32[]{:S(2)}, u32[]{:S(2)}) collective-permute-start(f32[32,448]{1,0:T(8,128)S(1)} %get-tuple-element.36), channel_id=1, source_target_pairs={{0,1},{1,0},{2,3},{3,2},{4,5},{5,4},{6,7},{7,6},{8,9},{9,8},{10,11... | collective-permute-start | bytes 172040 | tf_op jit(solution)/shard_map/ppermute | solution.py:343
  103.7 5.3 %collective-permute-start.15 = (f32[32,512]{1,0:T(8,128)S(1)}, f32[32,512]{1,0:T(8,128)S(1)}, u32[]{:S(2)}, u32[]{:S(2)}) collective-permute-start(f32[32,512]{1,0:T(8,128)S(1)} %get-tuple-element.41), channel_id=1, source_target_pairs={{0,1},{1,0},{2,3},{3,2},{4,5},{5,4},{6,7},{7,6},{8,9},{9,8},{10,11... | collective-permute-start | bytes 196616 | tf_op jit(solution)/shard_map/ppermute | solution.py:343
  103.8 6.6 %collective-permute-start.11 = (f32[32,448]{1,0:T(8,128)S(1)}, f32[32,448]{1,0:T(8,128)S(1)}, u32[]{:S(2)}, u32[]{:S(2)}) collective-permute-start(f32[32,448]{1,0:T(8,128)S(1)} %add.58), channel_id=1, source_target_pairs={{0,4},{1,5},{2,6},{3,7},{4,0},{5,1},{6,2},{7,3},{8,12},{9,13},{10,... | collective-permute-start | bytes 172040 | tf_op jit(solution)/shard_map/ppermute | solution.py:343
  105.5 21.8 %collective-permute-start.5 = (f32[192,384]{1,0:T(8,128)S(1)}, f32[192,384]{1,0:T(8,128)S(1)}, u32[]{:S(2)}, u32[]{:S(2)}) collective-permute-start(f32[192,384]{1,0:T(8,128)S(1)} %add.54), channel_id=1, source_target_pairs={{0,4},{1,5},{2,6},{3,7},{4,0},{5,1},{6,2},{7,3},{8,12},{9,13},{10,... | collective-permute-start | bytes 884744 | tf_op jit(solution)/shard_map/ppermute | solution.py:343
  106.0 21.8 %collective-permute-start.6 = (f32[192,384]{1,0:T(8,128)S(1)}, f32[192,384]{1,0:T(8,128)S(1)}, u32[]{:S(2)}, u32[]{:S(2)}) collective-permute-start(f32[192,384]{1,0:T(8,128)S(1)} %add.54), channel_id=1, source_target_pairs={{0,6},{1,7},{2,4},{3,5},{4,2},{5,3},{6,0},{7,1},{8,14},{9,15},{10,... | collective-permute-start | bytes 884744 | tf_op jit(solution)/shard_map/ppermute | solution.py:343
  108.5 19.4 %collective-permute-start.4 = (f32[192,384]{1,0:T(8,128)S(1)}, f32[192,384]{1,0:T(8,128)S(1)}, u32[]{:S(2)}, u32[]{:S(2)}) collective-permute-start(f32[192,384]{1,0:T(8,128)S(1)} %add.54), channel_id=1, source_target_pairs={{0,2},{1,3},{2,0},{3,1},{4,6},{5,7},{6,4},{7,5},{8,10},{9,11},{10,... | collective-permute-start | bytes 884744 | tf_op jit(solution)/shard_map/ppermute | solution.py:343
  109.0 15.2 %collective-permute-start.12 = (f32[32,448]{1,0:T(8,128)S(1)}, f32[32,448]{1,0:T(8,128)S(1)}, u32[]{:S(2)}, u32[]{:S(2)}) collective-permute-start(f32[32,448]{1,0:T(8,128)S(1)} %add.58), channel_id=1, source_target_pairs={{0,6},{1,7},{2,4},{3,5},{4,2},{5,3},{6,0},{7,1},{8,14},{9,15},{10,... | collective-permute-start | bytes 172040 | tf_op jit(solution)/shard_map/ppermute | solution.py:343
  110.5 15.3 %collective-permute-start.10 = (f32[32,448]{1,0:T(8,128)S(1)}, f32[32,448]{1,0:T(8,128)S(1)}, u32[]{:S(2)}, u32[]{:S(2)}) collective-permute-start(f32[32,448]{1,0:T(8,128)S(1)} %add.58), channel_id=1, source_target_pairs={{0,2},{1,3},{2,0},{3,1},{4,6},{5,7},{6,4},{7,5},{8,10},{9,11},{10,... | collective-permute-start | bytes 172040 | tf_op jit(solution)/shard_map/ppermute | solution.py:343
  124.3 4.8 %collective-permute-start.17 = (f32[32,512]{1,0:T(8,128)S(1)}, f32[32,512]{1,0:T(8,128)S(1)}, u32[]{:S(2)}, u32[]{:S(2)}) collective-permute-start(f32[32,512]{1,0:T(8,128)S(1)} %add.62), channel_id=1, source_target_pairs={{0,4},{1,5},{2,6},{3,7},{4,0},{5,1},{6,2},{7,3},{8,12},{9,13},{10,... | collective-permute-start | bytes 196616 | tf_op jit(solution)/shard_map/ppermute | solution.py:343
  125.8 5.2 %collective-permute-start.18 = (f32[32,512]{1,0:T(8,128)S(1)}, f32[32,512]{1,0:T(8,128)S(1)}, u32[]{:S(2)}, u32[]{:S(2)}) collective-permute-start(f32[32,512]{1,0:T(8,128)S(1)} %add.62), channel_id=1, source_target_pairs={{0,6},{1,7},{2,4},{3,5},{4,2},{5,3},{6,0},{7,1},{8,14},{9,15},{10,... | collective-permute-start | bytes 196616 | tf_op jit(solution)/shard_map/ppermute | solution.py:343
  127.2 4.3 %collective-permute-start.16 = (f32[32,512]{1,0:T(8,128)S(1)}, f32[32,512]{1,0:T(8,128)S(1)}, u32[]{:S(2)}, u32[]{:S(2)}) collective-permute-start(f32[32,512]{1,0:T(8,128)S(1)} %add.62), channel_id=1, source_target_pairs={{0,2},{1,3},{2,0},{3,1},{4,6},{5,7},{6,4},{7,5},{8,10},{9,11},{10,... | collective-permute-start | bytes 196616 | tf_op jit(solution)/shard_map/ppermute | solution.py:343
  127.9 3.9 %collective-permute-start.13 = (f32[32,448]{1,0:T(8,128)S(1)}, f32[32,448]{1,0:T(8,128)S(1)}, u32[]{:S(2)}, u32[]{:S(2)}) collective-permute-start(f32[32,448]{1,0:T(8,128)S(1)} %add_add_fusion.4.mine_ref), channel_id=1, source_target_pairs={{0,1},{1,0},{2,3},{3,2},{4,5},{5,4},{6,7},{7,6},{8,9},{9,8},{10,11... | collective-permute-start | bytes 172040 | tf_op jit(solution)/shard_map/ppermute | solution.py:343
  127.9 3.8 %collective-permute-start.7 = (f32[192,384]{1,0:T(8,128)S(1)}, f32[192,384]{1,0:T(8,128)S(1)}, u32[]{:S(2)}, u32[]{:S(2)}) collective-permute-start(f32[192,384]{1,0:T(8,128)S(1)} %add_add_fusion.gram_mine), channel_id=1, source_target_pairs={{0,1},{1,0},{2,3},{3,2},{4,5},{5,4},{6,7},{7,6},{8,9},{9,8},{10,11... | collective-permute-start | bytes 884744 | tf_op jit(solution)/shard_map/ppermute | solution.py:343
  131.6 1.3 collective-permute-start.19
  133.2 8.0 %collective-permute-start.21 = (f32[4,32,128]{2,1,0:T(8,128)S(1)}, f32[4,32,128]{2,1,0:T(8,128)S(1)}, u32[]{:S(2)}, u32[]{:S(2)}) collective-permute-start(f32[4,32,128]{2,1,0:T(8,128)S(1)} %first.1), channel_id=1, source_target_pairs={{0,16},{8,24},{16,0},{24,8},{1,17},{9,25},{17,1},{25,9},{2,18},{10... | collective-permute-start | bytes 196616 | tf_op jit(solution)/shard_map/ppermute | solution.py:343
  133.3 8.0 %collective-permute-start.22 = (f32[4,32,128]{2,1,0:T(8,128)S(1)}, f32[4,32,128]{2,1,0:T(8,128)S(1)}, u32[]{:S(2)}, u32[]{:S(2)}) collective-permute-start(f32[4,32,128]{2,1,0:T(8,128)S(1)} %first.1), channel_id=1, source_target_pairs={{0,24},{8,16},{16,8},{24,0},{1,25},{9,17},{17,9},{25,1},{2,26},{10... | collective-permute-start | bytes 196616 | tf_op jit(solution)/shard_map/ppermute | solution.py:343
  136.0 6.4 %collective-permute-start.20 = (f32[4,32,128]{2,1,0:T(8,128)S(1)}, f32[4,32,128]{2,1,0:T(8,128)S(1)}, u32[]{:S(2)}, u32[]{:S(2)}) collective-permute-start(f32[4,32,128]{2,1,0:T(8,128)S(1)} %first.1), channel_id=1, source_target_pairs={{0,8},{8,0},{16,24},{24,16},{1,9},{9,1},{17,25},{25,17},{2,10},{10... | collective-permute-start | bytes 196616 | tf_op jit(solution)/shard_map/ppermute | solution.py:343
  142.8 8.2 %collective-permute-start.24 = (f32[4,32,128]{2,1,0:T(8,128)S(1)}, f32[4,32,128]{2,1,0:T(8,128)S(1)}, u32[]{:S(2)}, u32[]{:S(2)}) collective-permute-start(f32[4,32,128]{2,1,0:T(8,128)S(1)} %second.1), channel_id=1, source_target_pairs={{0,16},{8,24},{16,0},{24,8},{1,17},{9,25},{17,1},{25,9},{2,18},{10... | collective-permute-start | bytes 196616 | tf_op jit(solution)/shard_map/ppermute | solution.py:343
  143.4 7.6 %collective-permute-start.25 = (f32[4,32,128]{2,1,0:T(8,128)S(1)}, f32[4,32,128]{2,1,0:T(8,128)S(1)}, u32[]{:S(2)}, u32[]{:S(2)}) collective-permute-start(f32[4,32,128]{2,1,0:T(8,128)S(1)} %second.1), channel_id=1, source_target_pairs={{0,24},{8,16},{16,8},{24,0},{1,25},{9,17},{17,9},{25,1},{2,26},{10... | collective-permute-start | bytes 196616 | tf_op jit(solution)/shard_map/ppermute | solution.py:343
  146.0 5.3 %collective-permute-start.23 = (f32[4,32,128]{2,1,0:T(8,128)S(1)}, f32[4,32,128]{2,1,0:T(8,128)S(1)}, u32[]{:S(2)}, u32[]{:S(2)}) collective-permute-start(f32[4,32,128]{2,1,0:T(8,128)S(1)} %second.1), channel_id=1, source_target_pairs={{0,8},{8,0},{16,24},{24,16},{1,9},{9,1},{17,25},{25,17},{2,10},{10... | collective-permute-start | bytes 196616 | tf_op jit(solution)/shard_map/ppermute | solution.py:343
  146.3 5.1 %collective-permute-start.27 = (f32[4,32,128]{2,1,0:T(8,128)S(1)}, f32[4,32,128]{2,1,0:T(8,128)S(1)}, u32[]{:S(2)}, u32[]{:S(2)}) collective-permute-start(f32[4,32,128]{2,1,0:T(8,128)S(1)} %add_add_fusion.2.image_ref.mine_ref), channel_id=1, source_target_pairs={{0,1},{1,0},{2,3},{3,2},{4,5},{5,4},{6,7},{7,6},{8,9},{9,8},{10,11... | collective-permute-start | bytes 196616 | tf_op jit(solution)/shard_map/ppermute | solution.py:343
  151.3 2.2 %collective-permute-start.26 = (f32[4,32,128]{2,1,0:T(8,128)S(1)}, f32[4,32,128]{2,1,0:T(8,128)S(1)}, u32[]{:S(2)}, u32[]{:S(2)}) collective-permute-start(f32[4,32,128]{2,1,0:T(8,128)S(1)} %add_add_fusion.1.mine_ref), channel_id=1, source_target_pairs={{0,1},{1,0},{2,3},{3,2},{4,5},{5,4},{6,7},{7,6},{8,9},{9,8},{10,11... | collective-permute-start | bytes 196616 | tf_op jit(solution)/shard_map/ppermute | solution.py:343

commit v3 on v2

--- a/solution.py
+++ b/solution.py
@@ -13,7 +13,7 @@
 VMEM = pl.BlockSpec(memory_space=pltpu.VMEM)
 ANY = pl.BlockSpec(memory_space=pl.ANY)
 ELIMINATE = 8
-PROJECT = 512
+PROJECT = 256
 
 
 def params(mib):
@@ -53,14 +53,17 @@
     ).astype(jnp.float32)
 
 
-def inverse_factor(squares):
+def inverse_factor(squares, beside=()):
     n = squares.shape[0]
     wide = 2 * n
     step = ELIMINATE
     start = jnp.concatenate([squares, eye(n)], axis=1)
     rows = [start[i : i + step] for i in range(0, n, step)]
     below = lax.broadcasted_iota(jnp.int32, (step, wide), 0)
+    beside = list(beside)
     for t in range(n // step):
+        if beside:
+            beside.pop(0)()
         columns = [
             {i: jnp.broadcast_to(rows[i][:, t * step + j : t * step + j + 1], (step, wide)) for i in range(t, n // step)}
             for j in range(step)
@@ -81,6 +84,8 @@
                     columns[m][i] = columns[m][i] - scaled[i] * across
         for i in range(t, n // step):
             rows[i] = rows[i] - update[i]
+    for call in beside:
+        call()
     done = jnp.concatenate(rows, axis=0)
     left, right = done[:, :n], done[:, n:]
     diagonal = jnp.sum(left * eye(n), axis=1, keepdims=True)
@@ -206,6 +211,38 @@
     )(part, *old)
 
 
+def late_kernel(shifts, piece_ref, basis_ref, *refs):
+    old, (high_ref, low_ref, mine_ref, other_ref, to_mine_ref, to_other_ref) = refs[:-6], refs[-6:]
+    new = halves(piece_ref[...])
+    high_ref[...], low_ref[...] = new
+    lower = cross([jnp.concatenate(pair, axis=0) for pair in zip(joined(old), new)], new).T
+    mine_ref[...], other_ref[...] = shares(lower)
+    side = lower.shape[1] - lower.shape[0]
+    basis, split = halves(in_turn(basis_ref, shifts)), halves(lower)
+    early = dot3([v[:, side:] for v in basis], [v[:, :side] for v in split], NN)
+    for ref, value in zip(
+        (to_mine_ref, to_other_ref), shares(jnp.concatenate([early, dot3(basis, split, NT)], axis=1))
+    ):
+        put(value, shifts, ref)
+
+
+def late(shifts, part, basis, old):
+    rows, width = part.shape
+    size = sum(piece.shape[0] for piece in old[::2]) + rows
+    fibres, ranks, modes = basis.shape
+    return pl.pallas_call(
+        functools.partial(late_kernel, shifts),
+        out_shape=(bf16(rows, width),) * 2 + (f32(rows // 2, size),) * 2 + (f32(fibres, ranks // 2, modes),) * 2,
+        in_specs=[VMEM] * (2 + len(old)),
+        out_specs=(VMEM,) * 6,
+        compiler_params=params(24),
+        cost_estimate=pl.CostEstimate(
+            flops=8 * rows * width * size, bytes_accessed=4 * width * size, transcendentals=0
+        ),
+        name="late",
+    )(part, basis, *old)
+
+
 def ranks_here(basis):
     half = basis.shape[0] // 2
     return jnp.where(low_core(), basis[:half], basis[half:])
@@ -221,14 +258,16 @@
     split = halves(gram)
     high_ref[...], low_ref[...] = split
     basis = halves(ranks_here(in_turn(basis_ref, shifts))[:, : gram.shape[0]])
-    image_ref[...] = dot3(basis, split, NN)
+    image = dot3(basis, split, NN)
+    rest = basis_ref.shape[0] * basis_ref.shape[2] - gram.shape[0]
+    put(jnp.concatenate([image, jnp.zeros((image.shape[0], rest), jnp.float32)], axis=1), shifts, image_ref)
 
 
 def assemble(shifts, basis, block, lower):
     size = lower[0].shape[1]
     return pl.pallas_call(
         functools.partial(assemble_kernel, shifts),
-        out_shape=(bf16(size, size), bf16(size, size), f32(basis.shape[1] // 2, size)),
+        out_shape=(bf16(size, size), bf16(size, size), f32(basis.shape[0], basis.shape[1] // 2, basis.shape[2])),
         in_specs=[VMEM] * 5,
         out_specs=(VMEM,) * 3,
         compiler_params=params(16),
@@ -241,23 +280,6 @@
     late = dot3(image, stripe, NT)
     early = early + dot3([v[:, side:] for v in image], [v[:, :side] for v in stripe], NN)
     return jnp.concatenate([early, late], axis=1)
-
-
-def first_kernel(shifts, basis_ref, image_ref, mine_ref, other_ref, out_ref):
-    basis = halves(ranks_here(in_turn(basis_ref, shifts)))
-    put(with_stripe(image_ref[...], basis, halves(merged(mine_ref[...], other_ref[...]))), shifts, out_ref)
-
-
-def first(shifts, basis, image, stripe):
-    fibres, ranks, rows = basis.shape
-    return pl.pallas_call(
-        functools.partial(first_kernel, shifts),
-        out_shape=f32(fibres, ranks // 2, rows),
-        in_specs=[VMEM] * 4,
-        out_specs=VMEM,
-        compiler_params=params(16),
-        name="first",
-    )(basis, image, *stripe)
 
 
 def second_kernel(shifts, image_ref, high_ref, low_ref, mine_ref, other_ref, out_ref):
@@ -297,25 +319,29 @@
 
 
 def close_kernel(shifts, mine_ref, other_ref, inverse_ref, *refs):
-    pieces, (core_ref, basis_ref, slab, sems) = refs[:-4], refs[-4:]
+    pieces, (core_ref, basis_ref, slab, basis_slab, sems) = refs[:-5], refs[-5:]
     first = inverse_ref[...]
     image = dot(first, merged(by_fibre(mine_ref), by_fibre(other_ref)), NN, HIGHEST)
     turned = dot(first, merged(in_turn(mine_ref, shifts), in_turn(other_ref, shifts)), NN, HIGHEST)
     parts = halves(turned)
-    inverse = inverse_factor(dot(image, image, NT, HIGHEST))
-    width = core_ref.shape[3]
+    width = slab.shape[1]
     chunk = min(PROJECT, width)
-    raw = []
-    for c in range(0, width, chunk):
+    raw = {}
+
+    def project(c):
         columns = [jnp.concatenate([ref[:, c : c + chunk] for ref in pieces[k::2]], axis=0) for k in range(2)]
-        raw.append(dot3(parts, columns, NN))
-    basis_ref[...] = dot(inverse, image, NN, HIGHEST)
+        raw[c] = dot3(parts, columns, NN)
+
+    steps = [functools.partial(project, c) for c in range(0, width, chunk)]
+    inverse = inverse_factor(dot(image, image, NT, HIGHEST), steps)
+    basis_slab[...] = dot(inverse, image, NN, HIGHEST)
+    stores = [pltpu.make_async_copy(basis_slab, basis_ref, sems.at[0])]
+    stores[0].start()
     split = halves(inverse)
-    stores = []
     for n, c in enumerate(range(0, width, chunk)):
-        slab[:, c : c + chunk] = dot3(split, halves(raw[n]), NN)
+        slab[:, c : c + chunk] = dot3(split, halves(raw[c]), NN)
         stores.append(
-            pltpu.make_async_copy(slab.at[:, pl.ds(c, chunk)], core_ref.at[:, 0, 0, pl.ds(c, chunk)], sems.at[n])
+            pltpu.make_async_copy(slab.at[:, pl.ds(c, chunk)], core_ref.at[:, 0, 0, pl.ds(c, chunk)], sems.at[n + 1])
         )
         stores[-1].start()
     for store in stores:
@@ -329,10 +355,11 @@
         functools.partial(close_kernel, shifts),
         out_shape=(f32(2 * half, 1, 1, width), f32(2 * half, fibres * rows)),
         in_specs=[VMEM] * (3 + len(pieces)),
-        out_specs=(ANY, VMEM),
+        out_specs=(ANY, ANY),
         scratch_shapes=[
             pltpu.VMEM((2 * half, width), jnp.float32),
-            pltpu.SemaphoreType.DMA((width // min(PROJECT, width),)),
+            pltpu.VMEM((2 * half, fibres * rows), jnp.float32),
+            pltpu.SemaphoreType.DMA((width // min(PROJECT, width) + 1,)),
         ],
         compiler_params=params(24),
         name="close",
@@ -403,11 +430,11 @@
     pieces += (high, low)
     lower = over_cols(*lower, n_cols)
     *gram, image = assemble(shifts, start, block, lower)
-    high, low, *lower = stripe(parts[last][1], pieces)
+    high, low, *lower, mine, other = late(shifts, parts[last][1], start, pieces)
     pieces += (high, low)
+    mine = over_chips(mine + swap(other, "cols", n_cols, 1), "cols", n_cols)
     lower = over_cols(*lower, n_cols)
-
-    mine = over_chips(first(shifts, start, image, lower), "fibre", n_fibre)
+    mine = over_chips(mine + image, "fibre", n_fibre)
     other = swap(mine, "cols", n_cols, 1)
     inverse = factor(mine, other)
     mine = second(shifts, mine, gram, lower)

time: 159 us -> 145 us (0.912)
  waiting for transfers between devices: 99.6 us -> 58 us
  starting transfers between devices: 28.8 us -> 46.3 us
  local copies, waits for them, and re-layouts: 1.24 us -> 8.61 us
    ppermute x28 -> x32, waiting for transfers between devices: 99.6 us -> 58 us  [swap(): return lax.ppermute(value, axis, [(i, i ^ bit) for i in range(size)])]
    ppermute x28 -> x32, starting transfers between devices: 28.8 us -> 46.3 us  [swap(): return lax.ppermute(value, axis, [(i, i ^ bit) for i in range(size)])]
    unnamed x4 -> x20, local copies, waits for them, and re-layouts: 1.23 us -> 8.6 us
    pallas_call x3, Pallas kernels: 3.62 us -> 5.4 us  [arrive(): pl.pallas_call(functools.partial(arrive_kernel, len(parts), len(old) // 2...]
    pallas_call x1, Pallas kernels: 0.28 us -> 1.96 us  [late(): pl.pallas_call(functools.partial(late_kernel, shifts), out_shape=(bf16(ro...]
    pallas_call x2 -> x1, Pallas kernels: 3.89 us -> 2.4 us  [stripe(): pl.pallas_call(stripe_kernel, out_shape=(bf16(rows, width),) * 2 + (f32(r...]
  transfers between devices with their start and end apart: 28 -> 32, of which waited for: 13 -> 11; matrix products, arithmetic and copies ran while one was open for 0% -> 1% of each run, Pallas kernels for 13% -> 15%
where the time goes in v3:
time: 145 us; the launch traced here: 144 us
  waiting for transfers between devices  58 us (40%)
  starting transfers between devices  46.3 us (32%)
  Pallas kernels  28.8 us (20%)
  local copies, waits for them, and re-layouts  8.61 us (6%)
    ppermute x32, waiting for transfers between devices, swap(): return lax.ppermute(value, axis, [(i, i ^ bit) for i in range(size)])  58 us
    ppermute x32, starting transfers between devices, swap(): return lax.ppermute(value, axis, [(i, i ^ bit) for i in range(size)])  46.3 us
    pallas_call x6, Pallas kernels, extract(): pl.pallas_call(functools.partial(extract_kernel, shift, row), out_shape=f...  12.1 us
    unnamed x20, local copies, waits for them, and re-layouts  8.6 us
    pallas_call x3, Pallas kernels, arrive(): pl.pallas_call(functools.partial(arrive_kernel, len(parts), len(old) // 2...  5.4 us
    pallas_call x1, Pallas kernels, close(): pl.pallas_call(functools.partial(close_kernel, shifts), out_shape=(f32(2...  3.95 us
  transfers between devices with their start and end apart: 32, of which 11 were waited for; matrix products, arithmetic and copies ran while one was open for 1% of the time, Pallas kernels for 15%

profile of v3, /device:TPU:0, one launch (start us, length us, event | category | flops | bytes accessed | tf_op | source)
XLA Modules:
  0.0 143.8 jit_solution(6037595531229501498)
XLA Ops:
  0.6 2.3 %extract.10 = f32[128,2048]{1,0:T(8,128)} custom-call(f32[128,1,4,2048]{3,2,1,0:T(4,128)} %tensor_ref.11), custom_call_target="tpu_custom_call" | custom-call | bytes 2097152 | tf_op jit(solution)/shard_map/extract/pallas_call | solution.py:105
  3.0 3.1 %collective-permute-start.3 = (f32[128,2048]{1,0:T(8,128)}, f32[128,2048]{1,0:T(8,128)}, u32[]{:S(2)}, u32[]{:S(2)}) collective-permute-start(f32[128,2048]{1,0:T(8,128)} %extract.10), channel_id=1, source_target_pairs={{0,8},{8,0},{16,24},{24,16},{1,9},{9,1},{17,25},{25,17},{2,10},{10... | collective-permute-start | bytes 3145736 | tf_op jit(solution)/shard_map/ppermute | solution.py:370
  6.1 1.9 %extract.8 = f32[64,2048]{1,0:T(8,128)} custom-call(f32[128,1,4,2048]{3,2,1,0:T(4,128)} %tensor_ref.11), custom_call_target="tpu_custom_call" | custom-call | bytes 1048576 | tf_op jit(solution)/shard_map/extract/pallas_call | solution.py:105
  8.0 2.5 %collective-permute-start.1 = (f32[64,2048]{1,0:T(8,128)}, f32[64,2048]{1,0:T(8,128)S(1)}, u32[]{:S(2)}, u32[]{:S(2)}) collective-permute-start(f32[64,2048]{1,0:T(8,128)} %extract.8), channel_id=1, source_target_pairs={{0,24},{8,16},{16,8},{24,0},{1,25},{9,17},{17,9},{25,1},{2,26},{10... | collective-permute-start | bytes 1572872 | tf_op jit(solution)/shard_map/ppermute | solution.py:370
  10.5 1.9 %extract.9 = f32[64,2048]{1,0:T(8,128)} custom-call(f32[128,1,4,2048]{3,2,1,0:T(4,128)} %tensor_ref.11), custom_call_target="tpu_custom_call" | custom-call | bytes 1048576 | tf_op jit(solution)/shard_map/extract/pallas_call | solution.py:105
  12.4 1.4 collective-permute-start.2
  13.8 1.9 %extract.11 = f32[64,2048]{1,0:T(8,128)} custom-call(f32[128,1,4,2048]{3,2,1,0:T(4,128)} %tensor_ref.11), custom_call_target="tpu_custom_call" | custom-call | bytes 1048576 | tf_op jit(solution)/shard_map/extract/pallas_call | solution.py:105
  15.7 0.9 collective-permute-start.4
  16.6 2.2 %extract.7.refs_0_ = f32[128,2048]{1,0:T(8,128)} custom-call(f32[128,1,4,2048]{3,2,1,0:T(4,128)} %tensor_ref.11), custom_call_target="tpu_custom_call" | custom-call | bytes 2097152 | tf_op jit(solution)/shard_map/extract/pallas_call | solution.py:105
  18.8 1.2 copy-done.7
  20.0 0.5 arrive.3
  20.6 23.5 %collective-permute-done.1.refs_0_ = f32[64,2048]{1,0:T(8,128)S(1)} collective-permute-done((f32[64,2048]{1,0:T(8,128)}, f32[64,2048]{1,0:T(8,128)S(1)}, u32[]{:S(2)}, u32[]{:S(2)}) %collective-permute-start.1) | collective-permute-done | bytes 524320 | tf_op jit(solution)/shard_map/ppermute | solution.py:370
  44.1 0.8 copy-done.8
  44.9 10.5 %collective-permute-done.2.refs_1_ = f32[64,2048]{1,0:T(8,128)} collective-permute-done((f32[64,2048]{1,0:T(8,128)}, f32[64,2048]{1,0:T(8,128)}, u32[]{:S(2)}, u32[]{:S(2)}) %collective-permute-start.2) | collective-permute-done | bytes 524320 | tf_op jit(solution)/shard_map/ppermute | solution.py:370
  55.5 1.0 copy-done.9
  56.5 1.8 %arrive.4 = (bf16[128,2048]{1,0:T(8,128)(2,1)S(1)}, bf16[128,2048]{1,0:T(8,128)(2,1)S(1)}, f32[256,256]{1,0:T(8,128)S(1)}) custom-call(f32[64,2048]{1,0:T(8,128)S(1)} %copy-done.9, f32[64,2048]{1,0:T(8,128)} %collective-permute-done.2.refs_1_, bf16[128,2048]{1,0:T(8,128)(2,1)S(1)} %get-tuple-element.27.refs_2_.refs_1_.refs_0_, ...), custom_call_target="tpu_custom_call" | custom-call | flops 536870912 | bytes 2097152 | tf_op jit(solution)/shard_map/arrive/pallas_call | solution.py:177
  58.4 3.0 %arrive.5 = (bf16[128,2048]{1,0:T(8,128)(2,1)S(1)}, bf16[128,2048]{1,0:T(8,128)(2,1)S(1)}, f32[192,384]{1,0:T(8,128)S(1)}, f32[192,384]{1,0:T(8,128)}) custom-call(f32[128,2048]{1,0:T(8,128)} %collective-permute-done.3.refs_0_, bf16[128,2048]{1,0:T(8,128)(2,1)S(1)} %get-tuple-element.27.refs_2_.refs_1_.refs_0_, ...), custom_call_target="tpu_custom_call" | custom-call | flops 805306368 | bytes 3145728 | tf_op jit(solution)/shard_map/arrive/pallas_call | solution.py:177
  61.4 0.8 copy-done.1
  62.2 0.8 copy-done.3
  63.0 0.8 copy-done.5
  63.8 1.9 %extract.6 = f32[64,2048]{1,0:T(8,128)} custom-call(f32[128,1,4,2048]{3,2,1,0:T(4,128)} %tensor_ref.11), custom_call_target="tpu_custom_call" | custom-call | bytes 1048576 | tf_op jit(solution)/shard_map/extract/pallas_call | solution.py:105
  65.7 15.3 %collective-permute-start = (f32[64,2048]{1,0:T(8,128)}, f32[64,2048]{1,0:T(8,128)S(1)}, u32[]{:S(2)}, u32[]{:S(2)}) collective-permute-start(f32[64,2048]{1,0:T(8,128)} %extract.6), channel_id=1, source_target_pairs={{0,16},{8,24},{16,0},{24,8},{1,17},{9,25},{17,1},{25,9},{2,18},{10... | collective-permute-start | bytes 1572872 | tf_op jit(solution)/shard_map/ppermute | solution.py:370
  81.0 1.0 add.73
  82.0 1.6 %collective-permute-start.11 = (f32[192,384]{1,0:T(8,128)S(1)}, f32[192,384]{1,0:T(8,128)S(1)}, u32[]{:S(2)}, u32[]{:S(2)}) collective-permute-start(f32[192,384]{1,0:T(8,128)S(1)} %add.73), channel_id=1, source_target_pairs={{0,4},{1,5},{2,6},{3,7},{4,0},{5,1},{6,2},{7,3},{8,12},{9,13},{10,... | collective-permute-start | bytes 884744 | tf_op jit(solution)/shard_map/ppermute | solution.py:370
  83.6 1.4 collective-permute-start.12
  85.0 0.5 collective-permute-start.10
  85.6 1.0 copy-done.2
  86.6 1.0 copy-done.4
  87.6 1.0 copy-done.6
  88.7 2.4 %stripe.1 = (bf16[64,2048]{1,0:T(8,128)(2,1)S(1)}, bf16[64,2048]{1,0:T(8,128)(2,1)S(1)}, f32[32,448]{1,0:T(8,128)S(1)}, f32[32,448]{1,0:T(8,128)S(1)}) custom-call(f32[64,2048]{1,0:T(8,128)} %collective-permute-done.4.piece_ref, bf16[128,2048]{1,0:T(8,128)(2,1)S(1)} %get-tuple-element.27.refs_2_.refs_1_.refs_0_, ...), custom_call_target="tpu_custom_call" | custom-call | flops 469762048 | bytes 3670016 | tf_op jit(solution)/shard_map/stripe/pallas_call | solution.py:201
  91.1 0.1 collective-permute-start.14
  91.2 13.8 %collective-permute-done.piece_ref = f32[64,2048]{1,0:T(8,128)S(1)} collective-permute-done((f32[64,2048]{1,0:T(8,128)}, f32[64,2048]{1,0:T(8,128)S(1)}, u32[]{:S(2)}, u32[]{:S(2)}) %collective-permute-start) | collective-permute-done | bytes 524320 | tf_op jit(solution)/shard_map/ppermute | solution.py:370
  105.0 2.0 %late.1 = (bf16[64,2048]{1,0:T(8,128)(2,1)S(1)}, bf16[64,2048]{1,0:T(8,128)(2,1)S(1)}, f32[32,512]{1,0:T(8,128)S(1)}, f32[32,512]{1,0:T(8,128)S(1)}, f32[4,32,12...) custom-call(f32[64,2048]{1,0:T(8,128)S(1)} %collective-permute-done.piece_ref, ...), custom_call_target="tpu_custom_call" | custom-call | flops 536870912 | bytes 4194304 | tf_op jit(solution)/shard_map/late/pallas_call | solution.py:233
  107.0 0.1 collective-permute-start.5
  107.1 1.6 %collective-permute-start.16 = (f32[32,448]{1,0:T(8,128)S(1)}, f32[32,448]{1,0:T(8,128)S(1)}, u32[]{:S(2)}, u32[]{:S(2)}) collective-permute-start(f32[32,448]{1,0:T(8,128)S(1)} %add.77), channel_id=1, source_target_pairs={{0,4},{1,5},{2,6},{3,7},{4,0},{5,1},{6,2},{7,3},{8,12},{9,13},{10,... | collective-permute-start | bytes 172040 | tf_op jit(solution)/shard_map/ppermute | solution.py:370
  108.7 1.4 collective-permute-start.17
  110.1 0.5 collective-permute-start.15
  110.8 0.5 collective-permute-start.22
  111.3 0.3 collective-permute-done.16
  111.7 2.9 %collective-permute-start.7 = (f32[4,32,128]{2,1,0:T(8,128)S(1)}, f32[4,32,128]{2,1,0:T(8,128)S(1)}, u32[]{:S(2)}, u32[]{:S(2)}) collective-permute-start(f32[4,32,128]{2,1,0:T(8,128)S(1)} %add.69), channel_id=1, source_target_pairs={{0,4},{1,5},{2,6},{3,7},{4,0},{5,1},{6,2},{7,3},{8,12},{9,13},{10,... | collective-permute-start | bytes 196616 | tf_op jit(solution)/shard_map/ppermute | solution.py:370
  114.5 1.4 collective-permute-start.8
  115.9 0.2 collective-permute-start.6
  116.1 0.1 collective-permute-start.18
  116.2 1.2 collective-permute-done.18.other_ref
  117.5 1.9 %collective-permute-start.24 = (f32[32,512]{1,0:T(8,128)S(1)}, f32[32,512]{1,0:T(8,128)S(1)}, u32[]{:S(2)}, u32[]{:S(2)}) collective-permute-start(f32[32,512]{1,0:T(8,128)S(1)} %add.85), channel_id=1, source_target_pairs={{0,4},{1,5},{2,6},{3,7},{4,0},{5,1},{6,2},{7,3},{8,12},{9,13},{10,... | collective-permute-start | bytes 196616 | tf_op jit(solution)/shard_map/ppermute | solution.py:370
  119.4 1.4 collective-permute-start.25
  120.8 0.5 assemble.1
  121.2 0.2 collective-permute-start.23
  121.5 0.1 collective-permute-start.20
  121.6 1.0 collective-permute-start.21
  122.6 2.4 %collective-permute-start.19 = (f32[4,32,128]{2,1,0:T(8,128)S(1)}, f32[4,32,128]{2,1,0:T(8,128)S(1)}, u32[]{:S(2)}, u32[]{:S(2)}) collective-permute-start(f32[4,32,128]{2,1,0:T(8,128)S(1)} %add_add_fusion.5), channel_id=1, source_target_pairs={{0,8},{8,0},{16,24},{24,16},{1,9},{9,1},{17,25},{25,17},{2,10},{10... | collective-permute-start | bytes 196616 | tf_op jit(solution)/shard_map/ppermute | solution.py:370
  125.1 0.5 collective-permute-done.23
  125.6 0.1 collective-permute-start.26
  125.7 2.6 %collective-permute-done.20 = f32[4,32,128]{2,1,0:T(8,128)S(1)} collective-permute-done((f32[4,32,128]{2,1,0:T(8,128)S(1)}, f32[4,32,128]{2,1,0:T(8,128)S(1)}, u32[]{:S(2)}, u32[]{:S(2)}) %collective-permute-start.20) | collective-permute-done | bytes 65568 | tf_op jit(solution)/shard_map/ppermute | solution.py:370
  128.2 0.7 collective-permute-done.19
  129.0 0.4 second.1
  129.4 1.5 %collective-permute-start.28 = (f32[4,32,128]{2,1,0:T(8,128)S(1)}, f32[4,32,128]{2,1,0:T(8,128)S(1)}, u32[]{:S(2)}, u32[]{:S(2)}) collective-permute-start(f32[4,32,128]{2,1,0:T(8,128)S(1)} %second.1), channel_id=1, source_target_pairs={{0,16},{8,24},{16,0},{24,8},{1,17},{9,25},{17,1},{25,9},{2,18},{10... | collective-permute-start | bytes 196616 | tf_op jit(solution)/shard_map/ppermute | solution.py:370
  130.8 1.5 %collective-permute-start.29 = (f32[4,32,128]{2,1,0:T(8,128)S(1)}, f32[4,32,128]{2,1,0:T(8,128)S(1)}, u32[]{:S(2)}, u32[]{:S(2)}) collective-permute-start(f32[4,32,128]{2,1,0:T(8,128)S(1)} %second.1), channel_id=1, source_target_pairs={{0,24},{8,16},{16,8},{24,0},{1,25},{9,17},{17,9},{25,1},{2,26},{10... | collective-permute-start | bytes 196616 | tf_op jit(solution)/shard_map/ppermute | solution.py:370
  132.4 0.6 collective-permute-start.27
  132.9 3.3 %collective-permute-done.28 = f32[4,32,128]{2,1,0:T(8,128)S(1)} collective-permute-done((f32[4,32,128]{2,1,0:T(8,128)S(1)}, f32[4,32,128]{2,1,0:T(8,128)S(1)}, u32[]{:S(2)}, u32[]{:S(2)}) %collective-permute-start.28) | collective-permute-done | bytes 65568 | tf_op jit(solution)/shard_map/ppermute | solution.py:370
  136.2 0.8 collective-permute-done.29
  137.0 0.6 collective-permute-done.27
  137.7 2.1 %factor.1.inverse_ref = f32[64,64]{1,0:T(8,128)S(1)} custom-call(f32[4,32,128]{2,1,0:T(8,128)S(1)} %add_add_fusion.3.image_ref.mine_ref, f32[4,32,128]{2,1,0:T(8,128)S(1)} %collective-permute-done.31.other_ref), custom_call_target="tpu_custom_call" | custom-call | flops 10485760 | bytes 131072 | tf_op jit(solution)/shard_map/factor/pallas_call | solution.py:310
  139.8 3.9 %close.1 = (f32[64,1,1,2048]{3,2,1,0:T(1,128)}, f32[64,512]{1,0:T(8,128)}) custom-call(f32[4,32,128]{2,1,0:T(8,128)S(1)} %add_add_fusion.1.mine_ref, f32[4,32,128]{2,1,0:T(8,128)S(1)} %collective-permute-done.30.other_ref, f32[64,64]{1,0:T(8,128)S(1)} %factor.1.inverse_ref, bf16[128,2048]{1,0:T(8,128)(2,1)S(1)} %get-tuple-element.27.refs_2_.refs_1_.refs_0_, ...), custom_call_target="tpu_custom_call" | custom-call | tf_op jit(solution)/shard_map/close/pallas_call | solution.py:354
  (46 shorter events, 0.5 us)
Async XLA Ops:
  0.6 90.6 %copy-start = (f32[512,64]{0,1:T(8,128)S(1)}, f32[512,64]{0,1:T(8,128)}, u32[]{:S(2)}) copy-start(f32[512,64]{0,1:T(8,128)} %param.3) | copy-start | bytes 393220
  3.0 55.4 %collective-permute-start.3 = (f32[128,2048]{1,0:T(8,128)}, f32[128,2048]{1,0:T(8,128)}, u32[]{:S(2)}, u32[]{:S(2)}) collective-permute-start(f32[128,2048]{1,0:T(8,128)} %extract.10), channel_id=1, source_target_pairs={{0,8},{8,0},{16,24},{24,16},{1,9},{9,1},{17,25},{25,17},{2,10},{10... | collective-permute-start | bytes 3145736 | tf_op jit(solution)/shard_map/ppermute | solution.py:370
  8.0 36.1 %collective-permute-start.1 = (f32[64,2048]{1,0:T(8,128)}, f32[64,2048]{1,0:T(8,128)S(1)}, u32[]{:S(2)}, u32[]{:S(2)}) collective-permute-start(f32[64,2048]{1,0:T(8,128)} %extract.8), channel_id=1, source_target_pairs={{0,24},{8,16},{16,8},{24,0},{1,25},{9,17},{17,9},{25,1},{2,26},{10... | collective-permute-start | bytes 1572872 | tf_op jit(solution)/shard_map/ppermute | solution.py:370
  12.4 43.1 %collective-permute-start.2 = (f32[64,2048]{1,0:T(8,128)}, f32[64,2048]{1,0:T(8,128)}, u32[]{:S(2)}, u32[]{:S(2)}) collective-permute-start(f32[64,2048]{1,0:T(8,128)} %extract.9), channel_id=1, source_target_pairs={{0,24},{8,16},{16,8},{24,0},{1,25},{9,17},{17,9},{25,1},{2,26},{10... | collective-permute-start | bytes 1572872 | tf_op jit(solution)/shard_map/ppermute | solution.py:370
  15.7 69.9 %collective-permute-start.4 = (f32[64,2048]{1,0:T(8,128)}, f32[64,2048]{1,0:T(8,128)}, u32[]{:S(2)}, u32[]{:S(2)}) collective-permute-start(f32[64,2048]{1,0:T(8,128)} %extract.11), channel_id=1, source_target_pairs={{0,16},{8,24},{16,0},{24,8},{1,17},{9,25},{17,1},{25,9},{2,18},{10... | collective-permute-start | bytes 1572872 | tf_op jit(solution)/shard_map/ppermute | solution.py:370
  18.8 1.2 copy-start.7
  44.1 0.8 copy-start.8
  55.5 1.0 copy-start.9
  61.4 0.8 copy-start.1
  62.2 0.8 copy-start.3
  63.0 0.8 copy-start.5
  63.8 17.2 %collective-permute-start.9 = (f32[192,384]{1,0:T(8,128)}, f32[192,384]{1,0:T(8,128)}, u32[]{:S(2)}, u32[]{:S(2)}) collective-permute-start(f32[192,384]{1,0:T(8,128)} %get-tuple-element.40), channel_id=1, source_target_pairs={{0,1},{1,0},{2,3},{3,2},{4,5},{5,4},{6,7},{7,6},{8,9},{9,8},{10,11... | collective-permute-start | bytes 884744 | tf_op jit(solution)/shard_map/ppermute | solution.py:370
  65.7 39.3 %collective-permute-start = (f32[64,2048]{1,0:T(8,128)}, f32[64,2048]{1,0:T(8,128)S(1)}, u32[]{:S(2)}, u32[]{:S(2)}) collective-permute-start(f32[64,2048]{1,0:T(8,128)} %extract.6), channel_id=1, source_target_pairs={{0,16},{8,24},{16,0},{24,8},{1,17},{9,25},{17,1},{25,9},{2,18},{10... | collective-permute-start | bytes 1572872 | tf_op jit(solution)/shard_map/ppermute | solution.py:370
  82.0 26.7 %collective-permute-start.11 = (f32[192,384]{1,0:T(8,128)S(1)}, f32[192,384]{1,0:T(8,128)S(1)}, u32[]{:S(2)}, u32[]{:S(2)}) collective-permute-start(f32[192,384]{1,0:T(8,128)S(1)} %add.73), channel_id=1, source_target_pairs={{0,4},{1,5},{2,6},{3,7},{4,0},{5,1},{6,2},{7,3},{8,12},{9,13},{10,... | collective-permute-start | bytes 884744 | tf_op jit(solution)/shard_map/ppermute | solution.py:370
  83.6 26.6 %collective-permute-start.12 = (f32[192,384]{1,0:T(8,128)S(1)}, f32[192,384]{1,0:T(8,128)S(1)}, u32[]{:S(2)}, u32[]{:S(2)}) collective-permute-start(f32[192,384]{1,0:T(8,128)S(1)} %add.73), channel_id=1, source_target_pairs={{0,6},{1,7},{2,4},{3,5},{4,2},{5,3},{6,0},{7,1},{8,14},{9,15},{10,... | collective-permute-start | bytes 884744 | tf_op jit(solution)/shard_map/ppermute | solution.py:370
  85.0 25.7 %collective-permute-start.10 = (f32[192,384]{1,0:T(8,128)S(1)}, f32[192,384]{1,0:T(8,128)S(1)}, u32[]{:S(2)}, u32[]{:S(2)}) collective-permute-start(f32[192,384]{1,0:T(8,128)S(1)} %add.73), channel_id=1, source_target_pairs={{0,2},{1,3},{2,0},{3,1},{4,6},{5,7},{6,4},{7,5},{8,10},{9,11},{10,... | collective-permute-start | bytes 884744 | tf_op jit(solution)/shard_map/ppermute | solution.py:370
  85.6 1.0 copy-start.2
  86.6 1.0 copy-start.4
  87.6 1.0 copy-start.6
  91.1 16.0 %collective-permute-start.14 = (f32[32,448]{1,0:T(8,128)S(1)}, f32[32,448]{1,0:T(8,128)S(1)}, u32[]{:S(2)}, u32[]{:S(2)}) collective-permute-start(f32[32,448]{1,0:T(8,128)S(1)} %get-tuple-element.42), channel_id=1, source_target_pairs={{0,1},{1,0},{2,3},{3,2},{4,5},{5,4},{6,7},{7,6},{8,9},{9,8},{10,11... | collective-permute-start | bytes 172040 | tf_op jit(solution)/shard_map/ppermute | solution.py:370
  107.0 3.8 %collective-permute-start.5 = (f32[4,32,128]{2,1,0:T(8,128)S(1)}, f32[4,32,128]{2,1,0:T(8,128)S(1)}, u32[]{:S(2)}, u32[]{:S(2)}) collective-permute-start(f32[4,32,128]{2,1,0:T(8,128)S(1)} %get-tuple-element.38), channel_id=1, source_target_pairs={{0,1},{1,0},{2,3},{3,2},{4,5},{5,4},{6,7},{7,6},{8,9},{9,8},{10,11... | collective-permute-start | bytes 196616 | tf_op jit(solution)/shard_map/ppermute | solution.py:370
  107.1 4.5 %collective-permute-start.16 = (f32[32,448]{1,0:T(8,128)S(1)}, f32[32,448]{1,0:T(8,128)S(1)}, u32[]{:S(2)}, u32[]{:S(2)}) collective-permute-start(f32[32,448]{1,0:T(8,128)S(1)} %add.77), channel_id=1, source_target_pairs={{0,4},{1,5},{2,6},{3,7},{4,0},{5,1},{6,2},{7,3},{8,12},{9,13},{10,... | collective-permute-start | bytes 172040 | tf_op jit(solution)/shard_map/ppermute | solution.py:370
  108.7 5.8 %collective-permute-start.17 = (f32[32,448]{1,0:T(8,128)S(1)}, f32[32,448]{1,0:T(8,128)S(1)}, u32[]{:S(2)}, u32[]{:S(2)}) collective-permute-start(f32[32,448]{1,0:T(8,128)S(1)} %add.77), channel_id=1, source_target_pairs={{0,6},{1,7},{2,4},{3,5},{4,2},{5,3},{6,0},{7,1},{8,14},{9,15},{10,... | collective-permute-start | bytes 172040 | tf_op jit(solution)/shard_map/ppermute | solution.py:370
  110.1 5.8 %collective-permute-start.15 = (f32[32,448]{1,0:T(8,128)S(1)}, f32[32,448]{1,0:T(8,128)S(1)}, u32[]{:S(2)}, u32[]{:S(2)}) collective-permute-start(f32[32,448]{1,0:T(8,128)S(1)} %add.77), channel_id=1, source_target_pairs={{0,2},{1,3},{2,0},{3,1},{4,6},{5,7},{6,4},{7,5},{8,10},{9,11},{10,... | collective-permute-start | bytes 172040 | tf_op jit(solution)/shard_map/ppermute | solution.py:370
  110.7 8.6 %collective-permute-start.13 = (f32[192,384]{1,0:T(8,128)S(1)}, f32[192,384]{1,0:T(8,128)S(1)}, u32[]{:S(2)}, u32[]{:S(2)}) collective-permute-start(f32[192,384]{1,0:T(8,128)S(1)} %add_add_fusion.gram_mine), channel_id=1, source_target_pairs={{0,1},{1,0},{2,3},{3,2},{4,5},{5,4},{6,7},{7,6},{8,9},{9,8},{10,11... | collective-permute-start | bytes 884744 | tf_op jit(solution)/shard_map/ppermute | solution.py:370
  110.8 5.3 %collective-permute-start.22 = (f32[32,512]{1,0:T(8,128)S(1)}, f32[32,512]{1,0:T(8,128)S(1)}, u32[]{:S(2)}, u32[]{:S(2)}) collective-permute-start(f32[32,512]{1,0:T(8,128)S(1)} %get-tuple-element.47), channel_id=1, source_target_pairs={{0,1},{1,0},{2,3},{3,2},{4,5},{5,4},{6,7},{7,6},{8,9},{9,8},{10,11... | collective-permute-start | bytes 196616 | tf_op jit(solution)/shard_map/ppermute | solution.py:370
  111.7 9.6 %collective-permute-start.7 = (f32[4,32,128]{2,1,0:T(8,128)S(1)}, f32[4,32,128]{2,1,0:T(8,128)S(1)}, u32[]{:S(2)}, u32[]{:S(2)}) collective-permute-start(f32[4,32,128]{2,1,0:T(8,128)S(1)} %add.69), channel_id=1, source_target_pairs={{0,4},{1,5},{2,6},{3,7},{4,0},{5,1},{6,2},{7,3},{8,12},{9,13},{10,... | collective-permute-start | bytes 196616 | tf_op jit(solution)/shard_map/ppermute | solution.py:370
  114.5 6.9 %collective-permute-start.8 = (f32[4,32,128]{2,1,0:T(8,128)S(1)}, f32[4,32,128]{2,1,0:T(8,128)S(1)}, u32[]{:S(2)}, u32[]{:S(2)}) collective-permute-start(f32[4,32,128]{2,1,0:T(8,128)S(1)} %add.69), channel_id=1, source_target_pairs={{0,6},{1,7},{2,4},{3,5},{4,2},{5,3},{6,0},{7,1},{8,14},{9,15},{10,... | collective-permute-start | bytes 196616 | tf_op jit(solution)/shard_map/ppermute | solution.py:370
  115.9 5.5 %collective-permute-start.6 = (f32[4,32,128]{2,1,0:T(8,128)S(1)}, f32[4,32,128]{2,1,0:T(8,128)S(1)}, u32[]{:S(2)}, u32[]{:S(2)}) collective-permute-start(f32[4,32,128]{2,1,0:T(8,128)S(1)} %add.69), channel_id=1, source_target_pairs={{0,2},{1,3},{2,0},{3,1},{4,6},{5,7},{6,4},{7,5},{8,10},{9,11},{10,... | collective-permute-start | bytes 196616 | tf_op jit(solution)/shard_map/ppermute | solution.py:370
  116.1 1.3 collective-permute-start.18
  117.5 5.2 %collective-permute-start.24 = (f32[32,512]{1,0:T(8,128)S(1)}, f32[32,512]{1,0:T(8,128)S(1)}, u32[]{:S(2)}, u32[]{:S(2)}) collective-permute-start(f32[32,512]{1,0:T(8,128)S(1)} %add.85), channel_id=1, source_target_pairs={{0,4},{1,5},{2,6},{3,7},{4,0},{5,1},{6,2},{7,3},{8,12},{9,13},{10,... | collective-permute-start | bytes 196616 | tf_op jit(solution)/shard_map/ppermute | solution.py:370
  119.4 5.7 %collective-permute-start.25 = (f32[32,512]{1,0:T(8,128)S(1)}, f32[32,512]{1,0:T(8,128)S(1)}, u32[]{:S(2)}, u32[]{:S(2)}) collective-permute-start(f32[32,512]{1,0:T(8,128)S(1)} %add.85), channel_id=1, source_target_pairs={{0,6},{1,7},{2,4},{3,5},{4,2},{5,3},{6,0},{7,1},{8,14},{9,15},{10,... | collective-permute-start | bytes 196616 | tf_op jit(solution)/shard_map/ppermute | solution.py:370
  121.2 4.3 %collective-permute-start.23 = (f32[32,512]{1,0:T(8,128)S(1)}, f32[32,512]{1,0:T(8,128)S(1)}, u32[]{:S(2)}, u32[]{:S(2)}) collective-permute-start(f32[32,512]{1,0:T(8,128)S(1)} %add.85), channel_id=1, source_target_pairs={{0,2},{1,3},{2,0},{3,1},{4,6},{5,7},{6,4},{7,5},{8,10},{9,11},{10,... | collective-permute-start | bytes 196616 | tf_op jit(solution)/shard_map/ppermute | solution.py:370
  121.5 6.7 %collective-permute-start.20 = (f32[4,32,128]{2,1,0:T(8,128)S(1)}, f32[4,32,128]{2,1,0:T(8,128)S(1)}, u32[]{:S(2)}, u32[]{:S(2)}) collective-permute-start(f32[4,32,128]{2,1,0:T(8,128)S(1)} %add_add_fusion.5), channel_id=1, source_target_pairs={{0,16},{8,24},{16,0},{24,8},{1,17},{9,25},{17,1},{25,9},{2,18},{10... | collective-permute-start | bytes 196616 | tf_op jit(solution)/shard_map/ppermute | solution.py:370
  121.6 6.7 %collective-permute-start.21 = (f32[4,32,128]{2,1,0:T(8,128)S(1)}, f32[4,32,128]{2,1,0:T(8,128)S(1)}, u32[]{:S(2)}, u32[]{:S(2)}) collective-permute-start(f32[4,32,128]{2,1,0:T(8,128)S(1)} %add_add_fusion.5), channel_id=1, source_target_pairs={{0,24},{8,16},{16,8},{24,0},{1,25},{9,17},{17,9},{25,1},{2,26},{10... | collective-permute-start | bytes 196616 | tf_op jit(solution)/shard_map/ppermute | solution.py:370
  122.6 6.3 %collective-permute-start.19 = (f32[4,32,128]{2,1,0:T(8,128)S(1)}, f32[4,32,128]{2,1,0:T(8,128)S(1)}, u32[]{:S(2)}, u32[]{:S(2)}) collective-permute-start(f32[4,32,128]{2,1,0:T(8,128)S(1)} %add_add_fusion.5), channel_id=1, source_target_pairs={{0,8},{8,0},{16,24},{24,16},{1,9},{9,1},{17,25},{25,17},{2,10},{10... | collective-permute-start | bytes 196616 | tf_op jit(solution)/shard_map/ppermute | solution.py:370
  125.6 3.4 %collective-permute-start.26 = (f32[32,512]{1,0:T(8,128)S(1)}, f32[32,512]{1,0:T(8,128)S(1)}, u32[]{:S(2)}, u32[]{:S(2)}) collective-permute-start(f32[32,512]{1,0:T(8,128)S(1)} %add_add_fusion.2.mine_ref), channel_id=1, source_target_pairs={{0,1},{1,0},{2,3},{3,2},{4,5},{5,4},{6,7},{7,6},{8,9},{9,8},{10,11... | collective-permute-start | bytes 196616 | tf_op jit(solution)/shard_map/ppermute | solution.py:370
  129.4 6.8 %collective-permute-start.28 = (f32[4,32,128]{2,1,0:T(8,128)S(1)}, f32[4,32,128]{2,1,0:T(8,128)S(1)}, u32[]{:S(2)}, u32[]{:S(2)}) collective-permute-start(f32[4,32,128]{2,1,0:T(8,128)S(1)} %second.1), channel_id=1, source_target_pairs={{0,16},{8,24},{16,0},{24,8},{1,17},{9,25},{17,1},{25,9},{2,18},{10... | collective-permute-start | bytes 196616 | tf_op jit(solution)/shard_map/ppermute | solution.py:370
  130.8 6.2 %collective-permute-start.29 = (f32[4,32,128]{2,1,0:T(8,128)S(1)}, f32[4,32,128]{2,1,0:T(8,128)S(1)}, u32[]{:S(2)}, u32[]{:S(2)}) collective-permute-start(f32[4,32,128]{2,1,0:T(8,128)S(1)} %second.1), channel_id=1, source_target_pairs={{0,24},{8,16},{16,8},{24,0},{1,25},{9,17},{17,9},{25,1},{2,26},{10... | collective-permute-start | bytes 196616 | tf_op jit(solution)/shard_map/ppermute | solution.py:370
  132.4 5.2 %collective-permute-start.27 = (f32[4,32,128]{2,1,0:T(8,128)S(1)}, f32[4,32,128]{2,1,0:T(8,128)S(1)}, u32[]{:S(2)}, u32[]{:S(2)}) collective-permute-start(f32[4,32,128]{2,1,0:T(8,128)S(1)} %second.1), channel_id=1, source_target_pairs={{0,8},{8,0},{16,24},{24,16},{1,9},{9,1},{17,25},{25,17},{2,10},{10... | collective-permute-start | bytes 196616 | tf_op jit(solution)/shard_map/ppermute | solution.py:370
  132.9 4.8 %collective-permute-start.31 = (f32[4,32,128]{2,1,0:T(8,128)S(1)}, f32[4,32,128]{2,1,0:T(8,128)S(1)}, u32[]{:S(2)}, u32[]{:S(2)}) collective-permute-start(f32[4,32,128]{2,1,0:T(8,128)S(1)} %add_add_fusion.3.image_ref.mine_ref), channel_id=1, source_target_pairs={{0,1},{1,0},{2,3},{3,2},{4,5},{5,4},{6,7},{7,6},{8,9},{9,8},{10,11... | collective-permute-start | bytes 196616 | tf_op jit(solution)/shard_map/ppermute | solution.py:370
  137.6 2.2 %collective-permute-start.30 = (f32[4,32,128]{2,1,0:T(8,128)S(1)}, f32[4,32,128]{2,1,0:T(8,128)S(1)}, u32[]{:S(2)}, u32[]{:S(2)}) collective-permute-start(f32[4,32,128]{2,1,0:T(8,128)S(1)} %add_add_fusion.1.mine_ref), channel_id=1, source_target_pairs={{0,1},{1,0},{2,3},{3,2},{4,5},{5,4},{6,7},{7,6},{8,9},{9,8},{10,11... | collective-permute-start | bytes 196616 | tf_op jit(solution)/shard_map/ppermute | solution.py:370
